TPU v7x, 32 devices: a whole 2x2x4 slice. The times are simulated.
32 devices in a mesh: groups: 2 (over y), seq: 1, mp: 8 (over z, x), section: 2 (over core).
Axes of the slice: x: 2, y: 2, z: 4, core: 2. Of those that a mesh axis runs over, the one named last changes fastest.
Arguments:
- latent: bfloat16 [1024, 3072], P(('groups', 'seq', 'section'), 'mp'), parts along dimension 0, may hold values from -6 to 6
- t_index: int32 [2], P('groups'), parts along dimension 0, may hold values from 0 to 27
- mod_table: bfloat16 [28, 3, 3072], P(None, None, 'mp'), may hold values from -1 to 4
- w_qkv: bfloat16 [3072, 6144], P('section', 'mp'), may hold values from -1 to 1
- w_out: bfloat16 [2048, 3072], P('section', 'mp'), may hold values from -0.125 to 0.125
Outputs:
- updated: bfloat16 [1024, 3072], P(('groups', 'seq', 'section'), 'mp'), parts along dimension 0
There are 2 independent parts, one for each index of `groups`. A program takes and returns all parts, laid end to end along the dimension named above; an argument that names none is the same for every part. Nothing has to cross between parts.
Inputs may be any that keep to these rules, and one draw needn't show every extreme that they name: `t_index`: the index of the current step among 28.
All inputs are finite; a program needn't handle non-finite values.
Results may differ from a plain program's by a relative error of at most 0.0085.
The roundings to bfloat16 on the way count: a program that leaves them out, or rounds other values in their place, can miss the bound.
Values may be sent and summed in bfloat16 or wider, within the bound.
A program may use at most 128 MiB of HBM per device.

v0:
```python
import functools
import math

import jax
import jax.numpy as jnp
from jax import lax
from jax.experimental import pallas as pl
from jax.experimental.pallas import tpu as pltpu
from jax.sharding import PartitionSpec as P

HEAD_DIM = 128
LANES = 128
WIDE = 2
CHUNKS = (2, 2)
MESH = pl.DeviceIdType.MESH


def layer_normed(values):
    mean_row = jnp.mean(values, axis=-1, keepdims=True)
    centred = values - mean_row
    variance = jnp.mean(centred * centred, axis=-1, keepdims=True)
    return centred * lax.rsqrt(variance + 1e-06)


def local(latent, t_index, mod_table, w_qkv, w_out):
    mod_local = lax.dynamic_index_in_dim(mod_table, t_index[0], 0, keepdims=False)
    features, mod_whole = (
        lax.all_gather(latent, "mp", axis=1, tiled=True),
        lax.all_gather(mod_local, "mp", axis=1, tiled=True),
    )
    mod_float = mod_whole.astype(jnp.float32)
    modulated = (
        layer_normed(features.astype(jnp.float32)) * (1.0 + mod_float[1]) + mod_float[0]
    ).astype(jnp.bfloat16)
    tok_rows = latent.shape[0]
    heads_dev = w_qkv.shape[1] // (3 * HEAD_DIM)
    qkv_full, out_full = (
        lax.all_gather(w_qkv, "section", axis=0, tiled=True),
        lax.all_gather(w_out, "section", axis=0, tiled=True),
    )
    projected = jnp.dot(modulated, qkv_full, preferred_element_type=jnp.float32).astype(
        jnp.bfloat16
    )
    grouped = projected.reshape(tok_rows, heads_dev, 3, HEAD_DIM)
    queries = grouped[:, :, 0]
    key_rows = grouped[:, :, 1]
    value_rows = grouped[:, :, 2]
    scale_factor = 1.0 / math.sqrt(HEAD_DIM)
    initial = (
        jnp.full((tok_rows, heads_dev), -1e30, jnp.float32),
        jnp.zeros((tok_rows, heads_dev), jnp.float32),
        jnp.zeros((tok_rows, heads_dev, HEAD_DIM), jnp.float32),
    )
    key_piece = lax.all_gather(key_rows, ("seq", "section"), axis=0, tiled=True)
    value_piece = lax.all_gather(value_rows, ("seq", "section"), axis=0, tiled=True)
    total_rows = key_piece.shape[0]
    block_rows = math.gcd(total_rows, 1024)

    def one_block(block_index, carried_block):
        running, totals, weighted = carried_block
        key_block = lax.dynamic_slice_in_dim(key_piece, block_index * block_rows, block_rows, 0)
        value_block = lax.dynamic_slice_in_dim(value_piece, block_index * block_rows, block_rows, 0)
        scores = (
            jnp.einsum("thd,khd->thk", queries, key_block, preferred_element_type=jnp.float32)
            * scale_factor
        )
        newest = jnp.maximum(running, jnp.max(scores, axis=-1))
        factor = jnp.exp(running - newest)
        weights = jnp.exp(scores - newest[..., None])
        totals = totals * factor + jnp.sum(weights, axis=-1)
        weighted = weighted * factor[..., None] + jnp.einsum(
            "thk,khd->thd",
            weights.astype(jnp.bfloat16),
            value_block,
            preferred_element_type=jnp.float32,
        )
        return (newest, totals, weighted)

    finished = lax.fori_loop(0, total_rows // block_rows, one_block, initial)
    attended = (
        (finished[2] / finished[1][..., None])
        .astype(jnp.bfloat16)
        .reshape(tok_rows, heads_dev * HEAD_DIM)
    )
    mixed_rows = jnp.dot(
        lax.all_gather(attended, "mp", axis=1, tiled=True),
        out_full,
        preferred_element_type=jnp.float32,
    )
    return (latent.astype(jnp.float32) + mod_local[2].astype(jnp.float32) * mixed_rows).astype(
        jnp.bfloat16
    )


def fused_kernel(
    n,
    x_hbm,
    t_ref,
    mod_hbm,
    wq_hbm,
    wo_hbm,
    out_ref,
    xs,
    table,
    small,
    wq,
    wo,
    acc,
    stat,
    proj,
    pkv,
    att,
    mixed,
    own_sem,
    table_sem,
    ssem,
    rsem,
    small_send,
    small_recv,
    wq_sem,
    wq_send,
    wo_sem,
    wo_send,
    kv_send,
    kv_recv,
):
    me = lax.axis_index("mp")
    sec = lax.axis_index("section")
    other = 1 - sec
    deep = n // WIDE
    z, x = me // WIDE, me % WIDE
    rows, feats = x_hbm.shape
    piece_q = wq.shape[1]
    per_sec = n // 2
    piece_o = wo.shape[1]
    heads = att.shape[2] // HEAD_DIM

    own_copy = pltpu.make_async_copy(x_hbm, xs.at[me], own_sem)
    own_copy.start()
    table_copy = pltpu.make_async_copy(mod_hbm, table, table_sem)
    table_copy.start()

    barrier = pltpu.get_barrier_semaphore()
    for step in range(1, n):
        pl.semaphore_signal(
            barrier, inc=1, device_id={"mp": lax.rem(me + step, n)}, device_id_type=MESH
        )
    pl.semaphore_signal(barrier, inc=1, device_id={"section": other}, device_id_type=MESH)

    def wq_local(i):
        p = sec * per_sec + i
        return pltpu.make_async_copy(
            wq_hbm.at[pl.ds(i * piece_q, piece_q)], wq.at[p], wq_sem.at[p]
        )

    def wo_local(i):
        return pltpu.make_async_copy(
            wo_hbm.at[pl.ds(i * piece_o, piece_o)],
            wo.at[sec * per_sec + i],
            wo_sem.at[sec * per_sec + i],
        )

    for i in range(per_sec):
        wq_local(i).start()
    for i in range(per_sec):
        wo_local(i).start()

    own_copy.wait()
    mine = xs[me].astype(jnp.float32)
    table_copy.wait()

    def mod_row(j):
        entries = table[j].astype(jnp.float32)
        steps = lax.broadcasted_iota(jnp.int32, entries.shape, 0)
        chosen = jnp.where(steps == t_ref[0], entries, 0.0)
        return jnp.sum(chosen, axis=0, keepdims=True)

    mean_col = jnp.sum(mine, axis=1, keepdims=True) * (1.0 / feats)
    off = mine - mean_col
    m2_col = jnp.sum(off * off, axis=1, keepdims=True)
    mean_row = jnp.broadcast_to(mean_col, (rows, LANES)).T[0:1, :]
    m2_row = jnp.broadcast_to(m2_col, (rows, LANES)).T[0:1, :]
    small[me, 0:1, :] = mod_row(0)
    small[me, 1:2, :] = 1.0 + mod_row(1)
    small[me, 2:3, 0:rows] = mean_row
    small[me, 3:4, 0:rows] = m2_row

    pl.semaphore_wait(barrier, n)

    def small_copy(step):
        return pltpu.make_async_remote_copy(
            src_ref=small.at[me],
            dst_ref=small.at[me],
            send_sem=small_send.at[step],
            recv_sem=small_recv.at[me],
            device_id={"mp": lax.rem(me + step, n)},
            device_id_type=MESH,
        )

    def chunk(phase, src, h):
        if phase == 0:
            part = rows // CHUNKS[0]
            return xs.at[src, pl.ds(h * part, part), :]
        split = CHUNKS[1] // heads
        part = rows // split
        return att.at[
            src, pl.ds(h % split * part, part), pl.ds(h // split * HEAD_DIM, HEAD_DIM)
        ]

    def route(src):
        sz, sx = src // WIDE, src % WIDE
        same = sx == x
        up = jnp.logical_and(same, jnp.logical_and(sz <= z, z + 1 < deep))
        down = jnp.logical_and(same, jnp.logical_and(sz >= z, z > 0))
        across = same
        return (
            (2, across, z * WIDE + (1 - x)),
            (0, up, me + WIDE),
            (1, down, me - WIDE),
        )

    def hop(phase, src, h, direction, target):
        return pltpu.make_async_remote_copy(
            src_ref=chunk(phase, src, h),
            dst_ref=chunk(phase, src, h),
            send_sem=ssem.at[phase, direction, src, h],
            recv_sem=rsem.at[phase, src, h],
            device_id={"mp": target},
            device_id_type=MESH,
        )

    def relay(phase, src, h):
        for direction, wanted, target in route(src):

            @pl.when(wanted)
            def _():
                hop(phase, src, h, direction, target).start()

    def arrive(phase, src, h):
        hop(phase, src, h, 0, me).wait_recv()
        relay(phase, src, h)

    relay(0, me, 0)
    for step in range(1, n):
        small_copy(step).start()
    for h in range(1, CHUNKS[0]):
        relay(0, me, h)

    def wq_remote(i):
        p = sec * per_sec + i
        return pltpu.make_async_remote_copy(
            src_ref=wq_hbm.at[pl.ds(i * piece_q, piece_q)],
            dst_ref=wq.at[p],
            send_sem=wq_send.at[i],
            recv_sem=wq_sem.at[p],
            device_id={"section": other},
            device_id_type=MESH,
        )

    def wo_remote(i):
        p = sec * per_sec + i
        return pltpu.make_async_remote_copy(
            src_ref=wo_hbm.at[pl.ds(i * piece_o, piece_o)],
            dst_ref=wo.at[p],
            send_sem=wo_send.at[i],
            recv_sem=wo_sem.at[p],
            device_id={"section": other},
            device_id_type=MESH,
        )

    for i in range(per_sec):
        wq_remote(i).start()
    for i in range(per_sec):
        wo_remote(i).start()

    def receive(phase, d):
        where = []
        for sign in (1, -1):
            sz = z + sign * d
            where.append((sz * WIDE + x, jnp.logical_and(sz >= 0, sz < deep)))
        for h in range(CHUNKS[phase]):
            for src, there in where:

                @pl.when(there)
                def _():
                    arrive(phase, src, h)

    def consume(phase, d, use):
        def one(i, carry_in):
            col = i < 2
            sign = 1 - 2 * lax.rem(i, 2)
            sz = z + sign * jnp.where(col, d, d - 1)
            there = jnp.logical_and(sz >= 0, sz < deep)
            there = jnp.logical_and(there, jnp.logical_or(i < 3, d > 1))
            src = sz * WIDE + jnp.where(col, x, 1 - x)

            @pl.when(jnp.logical_and(there, i >= 2))
            def _():
                for h in range(CHUNKS[phase]):
                    hop(phase, src, h, 0, me).wait_recv()

            @pl.when(there)
            def _():
                use(src)

            return carry_in

        lax.fori_loop(0, 4, one, 0)

    def sweep(phase, use):
        def early(d, carry):
            receive(phase, d)
            consume(phase, d - 1, use)
            return carry

        lax.fori_loop(2, deep, early, 0)
        consume(phase, deep - 1, use)
        consume(phase, deep, use)

    receive(0, 1)

    for step in range(1, n):
        p = lax.rem(me + step, n)
        pltpu.make_async_copy(small.at[p], small.at[p], small_recv.at[p]).wait()
    total = jnp.zeros((1, rows), jnp.float32)
    for p in range(n):
        total = total + small[p, 2:3, 0:rows]
    grand = total * (1.0 / n)
    m2 = jnp.zeros((1, rows), jnp.float32)
    for p in range(n):
        gap = small[p, 2:3, 0:rows] - grand
        m2 = m2 + small[p, 3:4, 0:rows] + feats * (gap * gap)
    inv = lax.rsqrt(m2 * (1.0 / (n * feats)) + 1e-06)
    stat[0] = jnp.broadcast_to(grand, (LANES, rows)).T
    stat[1] = jnp.broadcast_to(inv, (LANES, rows)).T

    def project(src):
        pltpu.make_async_copy(wq.at[src], wq.at[src], wq_sem.at[src]).wait()
        mean, rstd = stat[0], stat[1]
        shift_scale = small[src, 0:2, :]
        parts = []
        for c in range(feats // LANES):
            cols = slice(c * LANES, (c + 1) * LANES)
            values = xs[src, :, cols].astype(jnp.float32)
            parts.append(
                ((values - mean) * rstd * shift_scale[1:2, cols] + shift_scale[0:1, cols]).astype(
                    jnp.bfloat16
                )
            )
        return jnp.dot(
            jnp.concatenate(parts, axis=1), wq[src], preferred_element_type=jnp.float32
        )

    acc[...] = project(me)

    def use_projection(src):
        acc[...] += project(src)

    sweep(0, use_projection)

    def kv_copy(h):
        return pltpu.make_async_remote_copy(
            src_ref=proj.at[:, pl.ds((3 * h + 1) * HEAD_DIM, 2 * HEAD_DIM)],
            dst_ref=pkv.at[h],
            send_sem=kv_send.at[h],
            recv_sem=kv_recv.at[h],
            device_id={"section": other},
            device_id_type=MESH,
        )

    for h in range(heads):
        cols = slice((3 * h + 1) * HEAD_DIM, (3 * h + 3) * HEAD_DIM)
        proj[:, cols] = acc[:, cols].astype(jnp.bfloat16)
        kv_copy(h).start()

    factor = 1.0 / math.sqrt(HEAD_DIM)
    contract = (((1,), (1,)), ((), ()))
    for h in range(heads):
        base = 3 * h * HEAD_DIM
        queries = acc[:, base : base + HEAD_DIM].astype(jnp.bfloat16)
        own_k = proj[:, base + HEAD_DIM : base + 2 * HEAD_DIM]
        own_v = proj[:, base + 2 * HEAD_DIM : base + 3 * HEAD_DIM]
        s_own = lax.dot_general(queries, own_k, contract, preferred_element_type=jnp.float32) * factor
        kv_copy(h).wait_recv()
        far_k = pkv[h, :, 0:HEAD_DIM]
        far_v = pkv[h, :, HEAD_DIM : 2 * HEAD_DIM]
        s_far = lax.dot_general(queries, far_k, contract, preferred_element_type=jnp.float32) * factor
        top = jnp.maximum(
            jnp.max(s_own, axis=1, keepdims=True), jnp.max(s_far, axis=1, keepdims=True)
        )
        e_own = jnp.exp(s_own - top)
        e_far = jnp.exp(s_far - top)
        norm = jnp.sum(e_own, axis=1, keepdims=True) + jnp.sum(e_far, axis=1, keepdims=True)
        weighted = jnp.dot(
            e_own.astype(jnp.bfloat16), own_v, preferred_element_type=jnp.float32
        ) + jnp.dot(e_far.astype(jnp.bfloat16), far_v, preferred_element_type=jnp.float32)
        att[me, :, h * HEAD_DIM : (h + 1) * HEAD_DIM] = (weighted / norm).astype(jnp.bfloat16)
        for c in range(CHUNKS[1] // heads):
            relay(1, me, h * (CHUNKS[1] // heads) + c)

    def mix(src):
        pltpu.make_async_copy(wo.at[src], wo.at[src], wo_sem.at[src]).wait()
        return jnp.dot(att[src], wo[src], preferred_element_type=jnp.float32)

    receive(1, 1)
    mixed[...] = mix(me)

    def use_mix(src):
        mixed[...] += mix(src)

    sweep(1, use_mix)

    gate = mod_row(2)
    out_ref[...] = (xs[me].astype(jnp.float32) + gate * mixed[...]).astype(jnp.bfloat16)

    for step in range(1, n):
        small_copy(step).wait_send()
    for i in range(per_sec):
        wq_remote(i).wait_send()
        wo_remote(i).wait_send()
    for h in range(heads):
        kv_copy(h).wait_send()

    def drain(src, carry):
        for phase in range(2):
            for h in range(CHUNKS[phase]):
                for direction, wanted, target in route(src):

                    @pl.when(wanted)
                    def _():
                        hop(phase, src, h, direction, target).wait_send()

        return carry

    lax.fori_loop(0, n, drain, 0)


def fused(n, latent, t_index, mod_table, w_qkv, w_out):
    mod_table = jnp.transpose(mod_table, (1, 0, 2))
    rows, feats = latent.shape
    depth, cols = w_qkv.shape
    depth_o, cols_o = w_out.shape
    heads = cols // (3 * HEAD_DIM)
    bf, f32 = jnp.bfloat16, jnp.float32
    dma = pltpu.SemaphoreType.DMA
    return pl.pallas_call(
        functools.partial(fused_kernel, n),
        out_shape=jax.ShapeDtypeStruct((rows, feats), bf),
        in_specs=[
            pl.BlockSpec(memory_space=pltpu.HBM),
            pl.BlockSpec(memory_space=pltpu.SMEM),
            pl.BlockSpec(memory_space=pltpu.HBM),
            pl.BlockSpec(memory_space=pltpu.HBM),
            pl.BlockSpec(memory_space=pltpu.HBM),
        ],
        out_specs=pl.BlockSpec(memory_space=pltpu.VMEM),
        scratch_shapes=[
            pltpu.VMEM((n, rows, feats), bf),
            pltpu.VMEM(mod_table.shape, bf),
            pltpu.VMEM((n, 8, feats), f32),
            pltpu.VMEM((n, 2 * depth // n, cols), bf),
            pltpu.VMEM((n, 2 * depth_o // n, cols_o), bf),
            pltpu.VMEM((rows, cols), f32),
            pltpu.VMEM((2, rows, LANES), f32),
            pltpu.VMEM((rows, cols), bf),
            pltpu.VMEM((heads, rows, 2 * HEAD_DIM), bf),
            pltpu.VMEM((n, rows, heads * HEAD_DIM), bf),
            pltpu.VMEM((rows, cols_o), f32),
            dma,
            dma,
            dma((2, 3, n, max(CHUNKS))),
            dma((2, n, max(CHUNKS))),
            dma((n,)),
            dma((n,)),
            dma((n,)),
            dma((n // 2,)),
            dma((n,)),
            dma((n // 2,)),
            dma((heads,)),
            dma((heads,)),
        ],
        compiler_params=pltpu.CompilerParams(
            collective_id=0, has_side_effects=True, vmem_limit_bytes=60 * 1024 * 1024
        ),
    )(latent, t_index, mod_table, w_qkv, w_out)


def solution(mesh):
    in_specs = (
        P(("groups", "seq", "section"), "mp"),
        P("groups"),
        P(None, None, "mp"),
        P("section", "mp"),
        P("section", "mp"),
    )
    out_specs = P(("groups", "seq", "section"), "mp")
    n = mesh.shape["mp"]

    def body(latent, t_index, mod_table, w_qkv, w_out):
        heads = w_qkv.shape[1] // (3 * HEAD_DIM)
        fits = (
            mesh.shape["seq"] == 1
            and mesh.shape["section"] == 2
            and n % WIDE == 0
            and n > WIDE
            and heads == 2
            and latent.shape[0] <= latent.shape[1]
            and latent.shape[0] % 256 == 0
        )
        if not fits:
            return local(latent, t_index, mod_table, w_qkv, w_out)
        return fused(n, latent, t_index, mod_table, w_qkv, w_out)

    return jax.shard_map(body, mesh=mesh, in_specs=in_specs, out_specs=out_specs, check_vma=False)
```

profile of v0, /device:TPU:0, one launch (start us, length us, event | category | flops | bytes accessed | tf_op | source)
XLA Modules:
  0.0 46.9 jit_solution(955550869468892710)
XLA Ops:
  0.7 44.7 %shard_map.55 = bf16[256,384]{1,0:T(8,128)(2,1)} custom-call(bf16[256,384]{1,0:T(8,128)(2,1)} %x_hbm.1, s32[1]{0:T(128)S(6)} %copy.7.t_ref, bf16[3,28,384]{2,1,0:T(8,128)(2,1)} %bitcast.1, bf16[1536,768]{1,0:T(8,128)(2,1)} %wq_hbm.1, bf16[1024,384]{1,0:T(8,128)(2,1)} %wo_hbm.1), custom_call_target="tpu_custom_call" | custom-call | tf_op jit(solution)/shard_map/pallas_call | solution.py:446
  45.3 1.6 %copy.8 = bf16[256,384]{1,0:T(8,128)(2,1)} copy(bf16[256,384]{1,0:T(8,128)(2,1)} %shard_map.55) | data formatting | bytes 393216
where the time goes:
time: 47.1 us; the launch traced here: 46.9 us
  Pallas kernels  44.7 us (95%)
  local copies, waits for them, and re-layouts  1.62 us (3%)
  between operations  0.66 us (1%)
    pallas_call x1, Pallas kernels, fused(): pl.pallas_call(functools.partial(fused_kernel, n), out_shape=jax.ShapeDty...  44.7 us
    unnamed x1, local copies, waits for them, and re-layouts  1.62 us

commit v1 on v0

--- a/solution.py
+++ b/solution.py
@@ -445,7 +445,7 @@
     dma = pltpu.SemaphoreType.DMA
     return pl.pallas_call(
         functools.partial(fused_kernel, n),
-        out_shape=jax.ShapeDtypeStruct((rows, feats), bf),
+        out_shape=pltpu.VMEM((rows, feats), bf),
         in_specs=[
             pl.BlockSpec(memory_space=pltpu.HBM),
             pl.BlockSpec(memory_space=pltpu.SMEM),
@@ -480,9 +480,9 @@
             dma((heads,)),
         ],
         compiler_params=pltpu.CompilerParams(
-            collective_id=0, has_side_effects=True, vmem_limit_bytes=60 * 1024 * 1024
+            collective_id=0, has_side_effects=True, vmem_limit_bytes=24 * 1024 * 1024
         ),
-    )(latent, t_index, mod_table, w_qkv, w_out)
+    )(*(pltpu.with_memory_space_constraint(v, pltpu.HBM) if v.ndim > 1 else v for v in (latent, t_index, mod_table, w_qkv, w_out)))
 
 
 def solution(mesh):

time: 47.1 us -> 45.5 us (0.966)
  local copies, waits for them, and re-layouts: 1.62 us -> 0.68 us
  Pallas kernels: 44.7 us -> 44 us
    unnamed x1, local copies, waits for them, and re-layouts: 1.62 us -> 0.68 us
    pallas_call x1, Pallas kernels: 44.7 us -> 44 us  [fused(): pl.pallas_call(functools.partial(fused_kernel, n), out_shape=pltpu.VMEM((...]
where the time goes in v1:
time: 45.5 us; the launch traced here: 45.3 us
  Pallas kernels  44 us (97%)
  local copies, waits for them, and re-layouts  0.68 us (1%)
  between operations  0.66 us (1%)
    pallas_call x1, Pallas kernels, fused(): pl.pallas_call(functools.partial(fused_kernel, n), out_shape=pltpu.VMEM((...  44 us

profile of v1, /device:TPU:0, one launch (start us, length us, event | category | flops | bytes accessed | tf_op | source)
XLA Modules:
  0.0 45.3 jit_solution(9662571978305267352)
XLA Ops:
  0.7 44.0 %shard_map.55 = bf16[256,384]{1,0:T(8,128)(2,1)S(1)} custom-call(bf16[256,384]{1,0:T(8,128)(2,1)} %x_hbm.1, s32[1]{0:T(128)S(6)} %copy.8.t_ref, bf16[3,28,384]{2,1,0:T(8,128)(2,1)} %bitcast.1, bf16[1536,768]{1,0:T(8,128)(2,1)} %wq_hbm.1, bf16[1024,384]{1,0:T(8,128)(2,1)} %wo_hbm.1), custom_call_target="tpu_custom_call" | custom-call | tf_op jit(solution)/shard_map/pallas_call | solution.py:446
  44.6 0.7 %copy.7 = bf16[256,384]{1,0:T(8,128)(2,1)} copy(bf16[256,384]{1,0:T(8,128)(2,1)S(1)} %shard_map.55) | data formatting | bytes 393216

commit v2 on v1

v2 whole, which is shorter than its diff:
```python
import functools
import math

import jax
import jax.numpy as jnp
from jax import lax
from jax.experimental import pallas as pl
from jax.experimental.pallas import tpu as pltpu
from jax.sharding import PartitionSpec as P

HEAD_DIM = 128
LANES = 128
WIDE = 2
PIECES = 4
MESH = pl.DeviceIdType.MESH


def layer_normed(values):
    mean_row = jnp.mean(values, axis=-1, keepdims=True)
    centred = values - mean_row
    variance = jnp.mean(centred * centred, axis=-1, keepdims=True)
    return centred * lax.rsqrt(variance + 1e-06)


def local(latent, t_index, mod_table, w_qkv, w_out):
    mod_local = lax.dynamic_index_in_dim(mod_table, t_index[0], 0, keepdims=False)
    features, mod_whole = (
        lax.all_gather(latent, "mp", axis=1, tiled=True),
        lax.all_gather(mod_local, "mp", axis=1, tiled=True),
    )
    mod_float = mod_whole.astype(jnp.float32)
    modulated = (
        layer_normed(features.astype(jnp.float32)) * (1.0 + mod_float[1]) + mod_float[0]
    ).astype(jnp.bfloat16)
    tok_rows = latent.shape[0]
    heads_dev = w_qkv.shape[1] // (3 * HEAD_DIM)
    qkv_full, out_full = (
        lax.all_gather(w_qkv, "section", axis=0, tiled=True),
        lax.all_gather(w_out, "section", axis=0, tiled=True),
    )
    projected = jnp.dot(modulated, qkv_full, preferred_element_type=jnp.float32).astype(
        jnp.bfloat16
    )
    grouped = projected.reshape(tok_rows, heads_dev, 3, HEAD_DIM)
    queries = grouped[:, :, 0]
    key_rows = grouped[:, :, 1]
    value_rows = grouped[:, :, 2]
    scale_factor = 1.0 / math.sqrt(HEAD_DIM)
    initial = (
        jnp.full((tok_rows, heads_dev), -1e30, jnp.float32),
        jnp.zeros((tok_rows, heads_dev), jnp.float32),
        jnp.zeros((tok_rows, heads_dev, HEAD_DIM), jnp.float32),
    )
    key_piece = lax.all_gather(key_rows, ("seq", "section"), axis=0, tiled=True)
    value_piece = lax.all_gather(value_rows, ("seq", "section"), axis=0, tiled=True)
    total_rows = key_piece.shape[0]
    block_rows = math.gcd(total_rows, 1024)

    def one_block(block_index, carried_block):
        running, totals, weighted = carried_block
        key_block = lax.dynamic_slice_in_dim(key_piece, block_index * block_rows, block_rows, 0)
        value_block = lax.dynamic_slice_in_dim(value_piece, block_index * block_rows, block_rows, 0)
        scores = (
            jnp.einsum("thd,khd->thk", queries, key_block, preferred_element_type=jnp.float32)
            * scale_factor
        )
        newest = jnp.maximum(running, jnp.max(scores, axis=-1))
        factor = jnp.exp(running - newest)
        weights = jnp.exp(scores - newest[..., None])
        totals = totals * factor + jnp.sum(weights, axis=-1)
        weighted = weighted * factor[..., None] + jnp.einsum(
            "thk,khd->thd",
            weights.astype(jnp.bfloat16),
            value_block,
            preferred_element_type=jnp.float32,
        )
        return (newest, totals, weighted)

    finished = lax.fori_loop(0, total_rows // block_rows, one_block, initial)
    attended = (
        (finished[2] / finished[1][..., None])
        .astype(jnp.bfloat16)
        .reshape(tok_rows, heads_dev * HEAD_DIM)
    )
    mixed_rows = jnp.dot(
        lax.all_gather(attended, "mp", axis=1, tiled=True),
        out_full,
        preferred_element_type=jnp.float32,
    )
    return (latent.astype(jnp.float32) + mod_local[2].astype(jnp.float32) * mixed_rows).astype(
        jnp.bfloat16
    )


def item_codes(deep):
    def pack(d, sign, other, far):
        return ((d * 2 + (sign < 0)) * 2 + other) * 2 + far

    both = (1, -1)
    order = [pack(0, 1, 0, 0)] + [pack(1, sign, 0, 0) for sign in both] + [pack(0, 1, 1, 0)]
    for d in range(2, deep):
        order += [pack(d, sign, 0, 0) for sign in both]
        order += [pack(d - 1, sign, 1, 0) for sign in both]
    order += [pack(deep - 1, sign, 1, 0) for sign in both]
    far = [pack(d, sign, 1, 1) for d in range(1, deep) for sign in both]
    return order, far


def fused_kernel(
    n,
    x_hbm,
    t_ref,
    mod_hbm,
    wq_hbm,
    wo_hbm,
    out_ref,
    xs,
    table,
    small,
    gate,
    wq,
    wo,
    acc,
    stat,
    proj,
    pkv,
    att,
    mixed,
    own_sem,
    table_sem,
    ssem,
    rsem,
    small_send,
    small_recv,
    wq_sem,
    wq_send,
    wo_sem,
    wo_send,
    kv_send,
    kv_recv,
    wave,
):
    me = lax.axis_index("mp")
    sec = lax.axis_index("section")
    other = 1 - sec
    deep = n // WIDE
    z, x = me // WIDE, me % WIDE
    rows, feats = x_hbm.shape
    piece_q = wq.shape[1]
    per_sec = n // 2
    piece_o = wo.shape[1]
    heads = att.shape[1]
    half = rows // 2
    above = z + 1 < deep
    below = z > 0
    at_end = jnp.logical_or(z == 0, z == deep - 1)
    beside = z * WIDE + (1 - x)
    UP, DOWN, CROSS = 0, 1, 2
    targets = (me + WIDE, me - WIDE, beside)

    barrier = pltpu.get_barrier_semaphore()
    pl.semaphore_signal(barrier, inc=1, device_id={"mp": beside}, device_id_type=MESH)
    pl.semaphore_signal(barrier, inc=1, device_id={"section": other}, device_id_type=MESH)

    @pl.when(above)
    def _():
        pl.semaphore_signal(barrier, inc=1, device_id={"mp": me + WIDE}, device_id_type=MESH)

    @pl.when(below)
    def _():
        pl.semaphore_signal(barrier, inc=1, device_id={"mp": me - WIDE}, device_id_type=MESH)

    own_copy = pltpu.make_async_copy(x_hbm, xs.at[me], own_sem)
    own_copy.start()
    table_copy = pltpu.make_async_copy(mod_hbm, table, table_sem)
    table_copy.start()

    def wq_local(i):
        p = sec * per_sec + i
        return pltpu.make_async_copy(
            wq_hbm.at[pl.ds(i * piece_q, piece_q)], wq.at[p], wq_sem.at[p]
        )

    def wo_local(i):
        return pltpu.make_async_copy(
            wo_hbm.at[pl.ds(i * piece_o, piece_o)],
            wo.at[sec * per_sec + i],
            wo_sem.at[sec * per_sec + i],
        )

    def wq_remote(i):
        p = sec * per_sec + i
        return pltpu.make_async_remote_copy(
            src_ref=wq_hbm.at[pl.ds(i * piece_q, piece_q)],
            dst_ref=wq.at[p],
            send_sem=wq_send.at[i],
            recv_sem=wq_sem.at[p],
            device_id={"section": other},
            device_id_type=MESH,
        )

    def wo_remote(i):
        p = sec * per_sec + i
        return pltpu.make_async_remote_copy(
            src_ref=wo_hbm.at[pl.ds(i * piece_o, piece_o)],
            dst_ref=wo.at[p],
            send_sem=wo_send.at[i],
            recv_sem=wo_sem.at[p],
            device_id={"section": other},
            device_id_type=MESH,
        )

    def chunk(phase, src, q):
        if phase == 0:
            part = rows // PIECES
            return xs.at[src, pl.ds(pl.multiple_of(q * part, part), part), :]
        part = rows * heads // PIECES
        return att.at[
            src, lax.rem(q, heads), pl.ds(pl.multiple_of(q // heads * part, part), part), :
        ]

    def hop(phase, src, q, direction):
        return pltpu.make_async_remote_copy(
            src_ref=chunk(phase, src, q),
            dst_ref=chunk(phase, src, q),
            send_sem=ssem.at[phase, direction, src, q],
            recv_sem=rsem.at[phase, src, q],
            device_id={"mp": targets[direction]},
            device_id_type=MESH,
        )

    def own_hop(q, direction):
        part = rows // PIECES
        return pltpu.make_async_remote_copy(
            src_ref=x_hbm.at[pl.ds(q * part, part), :],
            dst_ref=chunk(0, me, q),
            send_sem=ssem.at[0, direction, me, q],
            recv_sem=rsem.at[0, me, q],
            device_id={"mp": targets[direction]},
            device_id_type=MESH,
        )

    def outward(start):
        start(CROSS)

        @pl.when(above)
        def _():
            start(UP)

        @pl.when(below)
        def _():
            start(DOWN)

    pl.semaphore_wait(barrier, 2 + above.astype(jnp.int32) + below.astype(jnp.int32))

    def tell(which, target):
        pl.semaphore_signal(
            wave.at[which], inc=1, device_id={"mp": target}, device_id_type=MESH
        )

    @pl.when(z == 0)
    def _():
        tell(UP, me + WIDE)

    @pl.when(z == deep - 1)
    def _():
        tell(DOWN, me - WIDE)

    for q in range(PIECES - 1):
        outward(lambda direction, q=q: own_hop(q, direction).start())

    for i in range(per_sec):
        wq_local(i).start()

    own_copy.wait()
    mine = xs[me].astype(jnp.float32)
    table_copy.wait()

    def mod_row(j):
        entries = table[j].astype(jnp.float32)
        steps = lax.broadcasted_iota(jnp.int32, entries.shape, 0)
        chosen = jnp.where(steps == t_ref[0], entries, 0.0)
        return jnp.sum(chosen, axis=0, keepdims=True)

    mean_col = jnp.sum(mine, axis=1, keepdims=True) * (1.0 / feats)
    off = mine - mean_col
    m2_col = jnp.sum(off * off, axis=1, keepdims=True)
    mean_row = jnp.broadcast_to(mean_col, (rows, LANES)).T[0:1, :]
    m2_row = jnp.broadcast_to(m2_col, (rows, LANES)).T[0:1, :]
    small[me, 0:1, :] = mod_row(0)
    small[me, 1:2, :] = 1.0 + mod_row(1)
    small[me, 2:3, 0:rows] = mean_row
    small[me, 3:4, 0:rows] = m2_row
    gate[0:1, :] = mod_row(2)

    def rise():
        @pl.when(below)
        def _():
            pl.semaphore_wait(wave.at[UP], 1)

            @pl.when(above)
            def _():
                tell(UP, me + WIDE)

    def sink():
        @pl.when(above)
        def _():
            pl.semaphore_wait(wave.at[DOWN], 1)

            @pl.when(below)
            def _():
                tell(DOWN, me - WIDE)

    @pl.when(2 * z < deep)
    def _():
        rise()
        sink()

    @pl.when(2 * z >= deep)
    def _():
        sink()
        rise()

    tell(CROSS, beside)
    pl.semaphore_wait(wave.at[CROSS], 1)

    def small_copy(step):
        return pltpu.make_async_remote_copy(
            src_ref=small.at[me, pl.ds(0, 4)],
            dst_ref=small.at[me, pl.ds(0, 4)],
            send_sem=small_send.at[step],
            recv_sem=small_recv.at[me],
            device_id={"mp": lax.rem(me + step, n)},
            device_id_type=MESH,
        )

    for step in range(1, n):
        small_copy(step).start()
    outward(lambda direction: own_hop(PIECES - 1, direction).start())
    for i in range(per_sec):
        wq_remote(i).start()
    for i in range(per_sec):
        wo_local(i).start()
        wo_remote(i).start()
    acc[...] = jnp.zeros_like(acc)
    mixed[...] = jnp.zeros_like(mixed)

    near = PIECES // 2
    order, far_order = item_codes(deep)

    def lookup(table_of, j):
        found = table_of[0]
        for i in range(1, len(table_of)):
            found = jnp.where(j == i, table_of[i], found)
        return found

    def inside(sz):
        return jnp.logical_and(sz >= 0, sz < deep)

    def is_end(sz):
        return jnp.logical_or(sz == 0, sz == deep - 1)

    def item(phase, code, use_all, use_half):
        far = lax.rem(code, 2) == 1
        there = lax.rem(code // 2, 2)
        sign = 1 - 2 * lax.rem(code // 4, 2)
        d = code // 8
        sz = z + sign * d
        end = is_end(sz)
        crossed = there == 1
        src = sz * WIDE + jnp.where(crossed, 1 - x, x)
        valid = jnp.logical_and(inside(sz), jnp.logical_or(jnp.logical_not(far), end))
        cross_near = jnp.logical_and(valid, jnp.logical_and(crossed, jnp.logical_not(far)))

        @pl.when(cross_near)
        def _():
            for q in range(near):
                hop(phase, src, q, CROSS).wait_recv()

        @pl.when(jnp.logical_and(cross_near, jnp.logical_not(end)))
        def _():
            for q in range(near, PIECES):
                hop(phase, src, q, CROSS).wait_recv()

        @pl.when(jnp.logical_and(jnp.logical_and(valid, far), d == deep - 1))
        def _():
            for q in range(near, PIECES):
                hop(phase, src, q, CROSS).wait_recv()

        split = jnp.logical_and(crossed, jnp.logical_and(end, d > 0))

        @pl.when(jnp.logical_and(valid, jnp.logical_not(split)))
        def _():
            use_all(src)

        @pl.when(jnp.logical_and(valid, split))
        def _():
            use_half(src, pl.multiple_of(jnp.where(far, half, 0), half))

    def passing(phase, s, q):
        late = q >= near

        @pl.when(jnp.logical_and(jnp.logical_and(s == 1, late), at_end))
        def _():
            hop(phase, beside, q, CROSS).wait_recv()

            @pl.when(z == 0)
            def _():
                hop(phase, beside, q, UP).start()

            @pl.when(z != 0)
            def _():
                hop(phase, beside, q, DOWN).start()

        for sign, onward, has in ((1, DOWN, below), (-1, UP, above)):
            sz = z + sign * s
            src = sz * WIDE + x

            @pl.when(inside(sz))
            def _():
                hop(phase, src, q, CROSS).wait_recv()

                @pl.when(has)
                def _():
                    hop(phase, src, q, onward).start()

                @pl.when(jnp.logical_not(jnp.logical_and(late, is_end(sz))))
                def _():
                    hop(phase, src, q, CROSS).start()

        for sign, onward in ((1, DOWN), (-1, UP)):
            sz = z + sign * (s - 1)
            src = sz * WIDE + (1 - x)

            @pl.when(
                jnp.logical_and(
                    jnp.logical_and(s > 1, late), jnp.logical_and(inside(sz), is_end(sz))
                )
            )
            def _():
                hop(phase, src, q, CROSS).wait_recv()
                hop(phase, src, q, onward).start()

    def drain(phase):
        def sent(src, direction, first, last):
            for q in range(first, last):
                hop(phase, src, q, direction).wait_send()

        outward(lambda direction: sent(me, direction, 0, PIECES))

        @pl.when(z == 0)
        def _():
            sent(beside, UP, near, PIECES)

        @pl.when(z == deep - 1)
        def _():
            sent(beside, DOWN, near, PIECES)

        def one(d, carry):
            for sign, onward, has in ((1, DOWN, below), (-1, UP, above)):
                sz = z + sign * d
                src = sz * WIDE + x
                across = sz * WIDE + (1 - x)

                @pl.when(inside(sz))
                def _():
                    sent(src, CROSS, 0, near)

                    @pl.when(jnp.logical_not(is_end(sz)))
                    def _():
                        sent(src, CROSS, near, PIECES)

                    @pl.when(has)
                    def _():
                        sent(src, onward, 0, PIECES)

                    @pl.when(jnp.logical_and(has, is_end(sz)))
                    def _():
                        sent(across, onward, near, PIECES)

            return carry

        lax.fori_loop(1, deep, one, 0)

    def sweep(phase, wait_steps, prepare, use_all, use_half, between):
        steps = (deep - 1) * PIECES
        done = steps - wait_steps

        def quiet(t, carry):
            passing(phase, 1 + t // PIECES, lax.rem(t, PIECES))
            return carry

        def busy(t, carry):
            item(phase, lookup(order[:done], t - wait_steps), use_all, use_half)
            passing(phase, 1 + t // PIECES, lax.rem(t, PIECES))
            return carry

        def rest(i, carry):
            item(phase, lookup(tail, i), use_all, use_half)
            return carry

        tail = order[done:] + far_order
        lax.fori_loop(0, wait_steps, quiet, 0)
        prepare()
        lax.fori_loop(wait_steps, steps, busy, 0)
        lax.fori_loop(0, len(tail) - 2, rest, 0)
        between()
        lax.fori_loop(len(tail) - 2, len(tail), rest, 0)

    def statistics():
        for p in range(n):
            pltpu.make_async_copy(wq.at[p], wq.at[p], wq_sem.at[p]).wait()
        for step in range(1, n):
            p = lax.rem(me + step, n)
            pltpu.make_async_copy(
                small.at[p, pl.ds(0, 4)], small.at[p, pl.ds(0, 4)], small_recv.at[p]
            ).wait()
        total = jnp.zeros((1, rows), jnp.float32)
        for p in range(n):
            total = total + small[p, 2:3, 0:rows]
        grand = total * (1.0 / n)
        m2 = jnp.zeros((1, rows), jnp.float32)
        for p in range(n):
            gap = small[p, 2:3, 0:rows] - grand
            m2 = m2 + small[p, 3:4, 0:rows] + feats * (gap * gap)
        inv = lax.rsqrt(m2 * (1.0 / (n * feats)) + 1e-06)
        stat[0] = jnp.broadcast_to(grand, (LANES, rows)).T
        stat[1] = jnp.broadcast_to(inv, (LANES, rows)).T

    def project(src, start, size):
        taken = pl.ds(start, size)
        mean, rstd = stat[0, taken, :], stat[1, taken, :]
        shift_scale = small[src, 0:2, :]
        parts = []
        for c in range(feats // LANES):
            cols = slice(c * LANES, (c + 1) * LANES)
            values = xs[src, taken, cols].astype(jnp.float32)
            parts.append(
                ((values - mean) * rstd * shift_scale[1:2, cols] + shift_scale[0:1, cols]).astype(
                    jnp.bfloat16
                )
            )
        acc[taken, :] += jnp.dot(
            jnp.concatenate(parts, axis=1), wq[src], preferred_element_type=jnp.float32
        )

    sweep(
        0,
        PIECES + PIECES // 2,
        statistics,
        lambda src: project(src, 0, rows),
        lambda src, start: project(src, start, half),
        lambda: None,
    )

    def kv_copy(h):
        return pltpu.make_async_remote_copy(
            src_ref=proj.at[:, pl.ds((3 * h + 1) * HEAD_DIM, 2 * HEAD_DIM)],
            dst_ref=pkv.at[h],
            send_sem=kv_send.at[h],
            recv_sem=kv_recv.at[h],
            device_id={"section": other},
            device_id_type=MESH,
        )

    for h in range(heads):
        cols = slice((3 * h + 1) * HEAD_DIM, (3 * h + 3) * HEAD_DIM)
        proj[:, cols] = acc[:, cols].astype(jnp.bfloat16)
        kv_copy(h).start()

    factor = 1.0 / math.sqrt(HEAD_DIM)
    contract = (((1,), (1,)), ((), ()))
    part = rows * heads // PIECES
    for q in range(PIECES):
        h, taken = q % heads, pl.ds(q // heads * part, part)
        base = 3 * h * HEAD_DIM
        queries = acc[taken, base : base + HEAD_DIM].astype(jnp.bfloat16)
        own_k = proj[:, base + HEAD_DIM : base + 2 * HEAD_DIM]
        own_v = proj[:, base + 2 * HEAD_DIM : base + 3 * HEAD_DIM]
        s_own = lax.dot_general(queries, own_k, contract, preferred_element_type=jnp.float32) * factor
        if q < heads:
            kv_copy(h).wait_recv()
        far_k = pkv[h, :, 0:HEAD_DIM]
        far_v = pkv[h, :, HEAD_DIM : 2 * HEAD_DIM]
        s_far = lax.dot_general(queries, far_k, contract, preferred_element_type=jnp.float32) * factor
        top = jnp.maximum(
            jnp.max(s_own, axis=1, keepdims=True), jnp.max(s_far, axis=1, keepdims=True)
        )
        e_own = jnp.exp(s_own - top)
        e_far = jnp.exp(s_far - top)
        norm = jnp.sum(e_own, axis=1, keepdims=True) + jnp.sum(e_far, axis=1, keepdims=True)
        weighted = jnp.dot(
            e_own.astype(jnp.bfloat16), own_v, preferred_element_type=jnp.float32
        ) + jnp.dot(e_far.astype(jnp.bfloat16), far_v, preferred_element_type=jnp.float32)
        att[me, h, taken, :] = (weighted / norm).astype(jnp.bfloat16)
        outward(lambda direction, q=q: hop(1, me, q, direction).start())

    def settle():
        for p in range(n):
            pltpu.make_async_copy(wo.at[p], wo.at[p], wo_sem.at[p]).wait()
        for step in range(1, n):
            small_copy(step).wait_send()
        for i in range(per_sec):
            wq_remote(i).wait_send()
            wo_remote(i).wait_send()
        for h in range(heads):
            kv_copy(h).wait_send()
        drain(0)

    def mix(src, start, size):
        taken = pl.ds(start, size)
        joined = jnp.concatenate([att[src, h, taken, :] for h in range(heads)], axis=1)
        mixed[taken, :] += jnp.dot(joined, wo[src], preferred_element_type=jnp.float32)

    settle()
    sweep(
        1,
        PIECES,
        lambda: None,
        lambda src: mix(src, 0, rows),
        lambda src, start: mix(src, start, half),
        lambda: drain(1),
    )

    out_ref[...] = (xs[me].astype(jnp.float32) + gate[0:1, :] * mixed[...]).astype(jnp.bfloat16)


def fused(n, latent, t_index, mod_table, w_qkv, w_out):
    mod_table = jnp.transpose(mod_table, (1, 0, 2))
    rows, feats = latent.shape
    depth, cols = w_qkv.shape
    depth_o, cols_o = w_out.shape
    heads = cols // (3 * HEAD_DIM)
    bf, f32 = jnp.bfloat16, jnp.float32
    dma = pltpu.SemaphoreType.DMA
    return pl.pallas_call(
        functools.partial(fused_kernel, n),
        out_shape=pltpu.VMEM((rows, feats), bf),
        in_specs=[
            pl.BlockSpec(memory_space=pltpu.HBM),
            pl.BlockSpec(memory_space=pltpu.SMEM),
            pl.BlockSpec(memory_space=pltpu.HBM),
            pl.BlockSpec(memory_space=pltpu.HBM),
            pl.BlockSpec(memory_space=pltpu.HBM),
        ],
        out_specs=pl.BlockSpec(memory_space=pltpu.VMEM),
        scratch_shapes=[
            pltpu.VMEM((n, rows, feats), bf),
            pltpu.VMEM(mod_table.shape, bf),
            pltpu.VMEM((n, 8, feats), f32),
            pltpu.VMEM((8, feats), f32),
            pltpu.VMEM((n, 2 * depth // n, cols), bf),
            pltpu.VMEM((n, 2 * depth_o // n, cols_o), bf),
            pltpu.VMEM((rows, cols), f32),
            pltpu.VMEM((2, rows, LANES), f32),
            pltpu.VMEM((rows, cols), bf),
            pltpu.VMEM((heads, rows, 2 * HEAD_DIM), bf),
            pltpu.VMEM((n, heads, rows, HEAD_DIM), bf),
            pltpu.VMEM((rows, cols_o), f32),
            dma,
            dma,
            dma((2, 3, n, PIECES)),
            dma((2, n, PIECES)),
            dma((n,)),
            dma((n,)),
            dma((n,)),
            dma((n // 2,)),
            dma((n,)),
            dma((n // 2,)),
            dma((heads,)),
            dma((heads,)),
            pltpu.SemaphoreType.REGULAR((3,)),
        ],
        compiler_params=pltpu.CompilerParams(
            collective_id=0, has_side_effects=True, vmem_limit_bytes=24 * 1024 * 1024
        ),
    )(*(pltpu.with_memory_space_constraint(v, pltpu.HBM) if v.ndim > 1 else v for v in (latent, t_index, mod_table, w_qkv, w_out)))


def solution(mesh):
    in_specs = (
        P(("groups", "seq", "section"), "mp"),
        P("groups"),
        P(None, None, "mp"),
        P("section", "mp"),
        P("section", "mp"),
    )
    out_specs = P(("groups", "seq", "section"), "mp")
    n = mesh.shape["mp"]

    def body(latent, t_index, mod_table, w_qkv, w_out):
        heads = w_qkv.shape[1] // (3 * HEAD_DIM)
        fits = (
            mesh.shape["seq"] == 1
            and mesh.shape["section"] == 2
            and n % WIDE == 0
            and n >= 3 * WIDE
            and heads == 2
            and latent.shape[0] <= latent.shape[1]
            and latent.shape[0] % 256 == 0
        )
        if not fits:
            return local(latent, t_index, mod_table, w_qkv, w_out)
        return fused(n, latent, t_index, mod_table, w_qkv, w_out)

    return jax.shard_map(body, mesh=mesh, in_specs=in_specs, out_specs=out_specs, check_vma=False)
```

time: 45.5 us -> 42.4 us (0.932)
  Pallas kernels: 44 us -> 40.9 us
    pallas_call x1, Pallas kernels: 44 us -> 40.9 us  [fused(): pl.pallas_call(functools.partial(fused_kernel, n), out_shape=pltpu.VMEM((...]
where the time goes in v2:
time: 42.4 us; the launch traced here: 42.2 us
  Pallas kernels  40.9 us (96%)
  local copies, waits for them, and re-layouts  0.68 us (2%)
  between operations  0.66 us (2%)
    pallas_call x1, Pallas kernels, fused(): pl.pallas_call(functools.partial(fused_kernel, n), out_shape=pltpu.VMEM((...  40.9 us

profile of v2, /device:TPU:0, one launch (start us, length us, event | category | flops | bytes accessed | tf_op | source)
XLA Modules:
  0.0 42.2 jit_solution(9152174247952567376)
XLA Ops:
  0.7 40.9 %shard_map.55 = bf16[256,384]{1,0:T(8,128)(2,1)S(1)} custom-call(bf16[256,384]{1,0:T(8,128)(2,1)} %x_hbm.1, s32[1]{0:T(128)S(6)} %copy.8.t_ref, bf16[3,28,384]{2,1,0:T(8,128)(2,1)} %bitcast.1, bf16[1536,768]{1,0:T(8,128)(2,1)} %wq_hbm.1, bf16[1024,384]{1,0:T(8,128)(2,1)} %wo_hbm.1), custom_call_target="tpu_custom_call" | custom-call | tf_op jit(solution)/shard_map/pallas_call | solution.py:636
  41.6 0.7 %copy.7 = bf16[256,384]{1,0:T(8,128)(2,1)} copy(bf16[256,384]{1,0:T(8,128)(2,1)S(1)} %shard_map.55) | data formatting | bytes 393216

commit v3 on v2

v3 whole, which is shorter than its diff:
```python
import functools
import math

import jax
import jax.numpy as jnp
from jax import lax
from jax.experimental import pallas as pl
from jax.experimental.pallas import tpu as pltpu
from jax.sharding import PartitionSpec as P

HEAD_DIM = 128
LANES = 128
WIDE = 2
PIECES = 4
MESH = pl.DeviceIdType.MESH


def layer_normed(values):
    mean_row = jnp.mean(values, axis=-1, keepdims=True)
    centred = values - mean_row
    variance = jnp.mean(centred * centred, axis=-1, keepdims=True)
    return centred * lax.rsqrt(variance + 1e-06)


def local(latent, t_index, mod_table, w_qkv, w_out):
    mod_local = lax.dynamic_index_in_dim(mod_table, t_index[0], 0, keepdims=False)
    features, mod_whole = (
        lax.all_gather(latent, "mp", axis=1, tiled=True),
        lax.all_gather(mod_local, "mp", axis=1, tiled=True),
    )
    mod_float = mod_whole.astype(jnp.float32)
    modulated = (
        layer_normed(features.astype(jnp.float32)) * (1.0 + mod_float[1]) + mod_float[0]
    ).astype(jnp.bfloat16)
    tok_rows = latent.shape[0]
    heads_dev = w_qkv.shape[1] // (3 * HEAD_DIM)
    qkv_full, out_full = (
        lax.all_gather(w_qkv, "section", axis=0, tiled=True),
        lax.all_gather(w_out, "section", axis=0, tiled=True),
    )
    projected = jnp.dot(modulated, qkv_full, preferred_element_type=jnp.float32).astype(
        jnp.bfloat16
    )
    grouped = projected.reshape(tok_rows, heads_dev, 3, HEAD_DIM)
    queries = grouped[:, :, 0]
    key_rows = grouped[:, :, 1]
    value_rows = grouped[:, :, 2]
    scale_factor = 1.0 / math.sqrt(HEAD_DIM)
    initial = (
        jnp.full((tok_rows, heads_dev), -1e30, jnp.float32),
        jnp.zeros((tok_rows, heads_dev), jnp.float32),
        jnp.zeros((tok_rows, heads_dev, HEAD_DIM), jnp.float32),
    )
    key_piece = lax.all_gather(key_rows, ("seq", "section"), axis=0, tiled=True)
    value_piece = lax.all_gather(value_rows, ("seq", "section"), axis=0, tiled=True)
    total_rows = key_piece.shape[0]
    block_rows = math.gcd(total_rows, 1024)

    def one_block(block_index, carried_block):
        running, totals, weighted = carried_block
        key_block = lax.dynamic_slice_in_dim(key_piece, block_index * block_rows, block_rows, 0)
        value_block = lax.dynamic_slice_in_dim(value_piece, block_index * block_rows, block_rows, 0)
        scores = (
            jnp.einsum("thd,khd->thk", queries, key_block, preferred_element_type=jnp.float32)
            * scale_factor
        )
        newest = jnp.maximum(running, jnp.max(scores, axis=-1))
        factor = jnp.exp(running - newest)
        weights = jnp.exp(scores - newest[..., None])
        totals = totals * factor + jnp.sum(weights, axis=-1)
        weighted = weighted * factor[..., None] + jnp.einsum(
            "thk,khd->thd",
            weights.astype(jnp.bfloat16),
            value_block,
            preferred_element_type=jnp.float32,
        )
        return (newest, totals, weighted)

    finished = lax.fori_loop(0, total_rows // block_rows, one_block, initial)
    attended = (
        (finished[2] / finished[1][..., None])
        .astype(jnp.bfloat16)
        .reshape(tok_rows, heads_dev * HEAD_DIM)
    )
    mixed_rows = jnp.dot(
        lax.all_gather(attended, "mp", axis=1, tiled=True),
        out_full,
        preferred_element_type=jnp.float32,
    )
    return (latent.astype(jnp.float32) + mod_local[2].astype(jnp.float32) * mixed_rows).astype(
        jnp.bfloat16
    )


def item_codes(deep):
    def pack(d, other, far):
        return (d * 2 + other) * 2 + far

    order = [pack(0, 0, 0), pack(1, 0, 0), pack(0, 1, 0)]
    for d in range(2, deep):
        order += [pack(d, 0, 0), pack(d - 1, 1, 0)]
    order.append(pack(deep - 1, 1, 0))
    return order, [pack(d, 1, 1) for d in range(1, deep)]


def fused_kernel(
    n,
    x_hbm,
    t_ref,
    mod_hbm,
    wq_hbm,
    wo_hbm,
    out_ref,
    xs,
    table,
    mods,
    sums,
    gate,
    wq,
    wo,
    acc,
    stat,
    proj,
    pkv,
    att,
    mixed,
    own_sem,
    table_sem,
    ssem,
    rsem,
    mods_send,
    mods_recv,
    sums_send,
    sums_recv,
    wq_sem,
    wq_send,
    wo_sem,
    wo_send,
    kv_send,
    kv_recv,
    wave,
):
    me = lax.axis_index("mp")
    sec = lax.axis_index("section")
    other = 1 - sec
    deep = n // WIDE
    z, x = me // WIDE, me % WIDE
    rows, feats = x_hbm.shape
    piece_q = wq.shape[1]
    per_sec = n // 2
    piece_o = wo.shape[1]
    heads = wo.shape[1] // HEAD_DIM
    half = rows // 2
    above = z + 1 < deep
    below = z > 0
    at_end = jnp.logical_or(z == 0, z == deep - 1)
    beside = z * WIDE + (1 - x)
    UP, DOWN, CROSS = 0, 1, 2
    targets = (me + WIDE, me - WIDE, beside)

    barrier = pltpu.get_barrier_semaphore()
    pl.semaphore_signal(barrier, inc=1, device_id={"mp": beside}, device_id_type=MESH)
    pl.semaphore_signal(barrier, inc=1, device_id={"section": other}, device_id_type=MESH)

    @pl.when(above)
    def _():
        pl.semaphore_signal(barrier, inc=1, device_id={"mp": me + WIDE}, device_id_type=MESH)

    @pl.when(below)
    def _():
        pl.semaphore_signal(barrier, inc=1, device_id={"mp": me - WIDE}, device_id_type=MESH)

    own_copy = pltpu.make_async_copy(x_hbm, xs.at[pl.ds(me * rows, rows)], own_sem)
    own_copy.start()
    table_copy = pltpu.make_async_copy(mod_hbm, table, table_sem)
    table_copy.start()

    def wq_local(i):
        p = sec * per_sec + i
        return pltpu.make_async_copy(
            wq_hbm.at[pl.ds(i * piece_q, piece_q)], wq.at[p], wq_sem
        )

    def wo_local(i):
        return pltpu.make_async_copy(
            wo_hbm.at[pl.ds(i * piece_o, piece_o)],
            wo.at[sec * per_sec + i],
            wo_sem,
        )

    def wq_remote(i):
        p = sec * per_sec + i
        return pltpu.make_async_remote_copy(
            src_ref=wq_hbm.at[pl.ds(i * piece_q, piece_q)],
            dst_ref=wq.at[p],
            send_sem=wq_send,
            recv_sem=wq_sem,
            device_id={"section": other},
            device_id_type=MESH,
        )

    def wo_remote(i):
        p = sec * per_sec + i
        return pltpu.make_async_remote_copy(
            src_ref=wo_hbm.at[pl.ds(i * piece_o, piece_o)],
            dst_ref=wo.at[p],
            send_sem=wo_send,
            recv_sem=wo_sem,
            device_id={"section": other},
            device_id_type=MESH,
        )

    parts = (rows // PIECES, rows * heads // PIECES)

    def chunk(phase, src, q):
        part = parts[phase]
        if phase == 0:
            return xs.at[pl.ds(pl.multiple_of(src * rows + q * part, part), part), :]
        first = (src * heads + lax.rem(q, heads)) * rows + q // heads * part
        return att.at[pl.ds(pl.multiple_of(first, part), part), :]

    def hop(phase, src, q, direction):
        return pltpu.make_async_remote_copy(
            src_ref=chunk(phase, src, q),
            dst_ref=chunk(phase, src, q),
            send_sem=ssem.at[phase, direction],
            recv_sem=rsem.at[phase, src, q],
            device_id={"mp": targets[direction]},
            device_id_type=MESH,
        )

    near = PIECES // 2

    def own_along(phase, slot):
        q = lax.rem(slot + jnp.where(at_end, near, 0), PIECES)

        @pl.when(above)
        def _():
            hop(phase, me, q, UP).start()

        @pl.when(below)
        def _():
            hop(phase, me, q, DOWN).start()

    pl.semaphore_wait(barrier, 2 + above.astype(jnp.int32) + below.astype(jnp.int32))

    def tell(which, target):
        pl.semaphore_signal(
            wave.at[which], inc=1, device_id={"mp": target}, device_id_type=MESH
        )

    @pl.when(z == 0)
    def _():
        tell(UP, me + WIDE)

    @pl.when(z == deep - 1)
    def _():
        tell(DOWN, me - WIDE)

    def rise():
        @pl.when(below)
        def _():
            pl.semaphore_wait(wave.at[UP], 1)

            @pl.when(above)
            def _():
                tell(UP, me + WIDE)

    def sink():
        @pl.when(above)
        def _():
            pl.semaphore_wait(wave.at[DOWN], 1)

            @pl.when(below)
            def _():
                tell(DOWN, me - WIDE)

    own_copy.wait()
    for slot in range(PIECES - 1):
        hop(0, me, slot, CROSS).start()
        own_along(0, slot)

    for i in range(per_sec):
        wq_local(i).start()

    @pl.when(2 * z < deep)
    def _():
        rise()

    @pl.when(2 * z >= deep)
    def _():
        sink()

    mine = xs[pl.ds(me * rows, rows), :].astype(jnp.float32)
    table_copy.wait()

    def mod_row(j):
        entries = table[j].astype(jnp.float32)
        steps = lax.broadcasted_iota(jnp.int32, entries.shape, 0)
        chosen = jnp.where(steps == t_ref[0], entries, 0.0)
        return jnp.sum(chosen, axis=0, keepdims=True)

    mean_col = jnp.sum(mine, axis=1, keepdims=True) * (1.0 / feats)
    off = mine - mean_col
    m2_col = jnp.sum(off * off, axis=1, keepdims=True)
    mean_row = jnp.broadcast_to(mean_col, (rows, LANES)).T[0:1, :]
    m2_row = jnp.broadcast_to(m2_col, (rows, LANES)).T[0:1, :]
    mods[me, 0:2, :] = jnp.concatenate([mod_row(0), mod_row(1)], axis=0).astype(jnp.bfloat16)
    sums[me, 0:1, :] = mean_row
    sums[me, 1:2, :] = m2_row
    gate[0:1, :] = mod_row(2)

    @pl.when(2 * z < deep)
    def _():
        sink()

    @pl.when(2 * z >= deep)
    def _():
        rise()

    tell(CROSS, beside)
    pl.semaphore_wait(wave.at[CROSS], 1)

    def small_copies(step):
        return [
            pltpu.make_async_remote_copy(
                src_ref=held.at[me, pl.ds(0, 2)],
                dst_ref=held.at[me, pl.ds(0, 2)],
                send_sem=send_sem,
                recv_sem=recv_sem,
                device_id={"mp": lax.rem(me + step, n)},
                device_id_type=MESH,
            )
            for held, send_sem, recv_sem in (
                (sums, sums_send, sums_recv),
                (mods, mods_send, mods_recv),
            )
        ]

    def settled(ref, sem):
        pltpu.make_async_copy(ref, ref, sem).wait()

    for step in range(1, n):
        for copy in small_copies(step):
            copy.start()
    hop(0, me, PIECES - 1, CROSS).start()
    own_along(0, PIECES - 1)
    for i in range(per_sec):
        wq_remote(i).start()
    for i in range(per_sec):
        wo_local(i).start()
        wo_remote(i).start()
    acc[...] = jnp.zeros_like(acc)
    mixed[...] = jnp.zeros_like(mixed)

    order, far_order = item_codes(deep)

    def lookup(table_of, j):
        found = table_of[0]
        for i in range(1, len(table_of)):
            found = jnp.where(j == i, table_of[i], found)
        return found

    def inside(sz):
        return jnp.logical_and(sz >= 0, sz < deep)

    def is_end(sz):
        return jnp.logical_or(sz == 0, sz == deep - 1)

    def item(phase, code, use_all, use_half):
        far = lax.rem(code, 2) == 1
        crossed = lax.rem(code // 2, 2) == 1
        d = code // 4

        def one(i, carry):
            sz = z + (1 - 2 * i) * d
            end = is_end(sz)
            src = sz * WIDE + jnp.where(crossed, 1 - x, x)
            valid = jnp.logical_and(inside(sz), jnp.logical_or(jnp.logical_not(far), end))
            valid = jnp.logical_and(valid, jnp.logical_or(d > 0, i == 0))
            direct = jnp.logical_and(valid, jnp.logical_and(crossed, jnp.logical_not(far)))

            @pl.when(direct)
            def _():
                for q in range(near, PIECES):
                    hop(phase, src, q, CROSS).wait_recv()

            @pl.when(jnp.logical_and(direct, jnp.logical_not(end)))
            def _():
                for q in range(near):
                    hop(phase, src, q, CROSS).wait_recv()

            @pl.when(jnp.logical_and(jnp.logical_and(valid, far), d == deep - 1))
            def _():
                for q in range(near):
                    hop(phase, src, q, CROSS).wait_recv()

            split = jnp.logical_and(crossed, jnp.logical_and(end, d > 0))

            @pl.when(jnp.logical_and(valid, jnp.logical_not(split)))
            def _():
                use_all(src)

            @pl.when(jnp.logical_and(valid, split))
            def _():
                use_half(src, pl.multiple_of(jnp.where(far, 0, half), half))

            return carry

        lax.fori_loop(0, 2, one, 0)

    def passing(phase, t):
        s, slot = 1 + t // PIECES, lax.rem(t, PIECES)
        for sign, onward, has in ((1, DOWN, below), (-1, UP, above)):
            sz = z + sign * s
            src = sz * WIDE + x
            end = is_end(sz)
            q = lax.rem(slot + jnp.where(end, near, 0), PIECES)

            @pl.when(inside(sz))
            def _():
                hop(phase, src, q, CROSS).wait_recv()

                @pl.when(has)
                def _():
                    hop(phase, src, q, onward).start()

                @pl.when(jnp.logical_not(jnp.logical_and(q < near, end)))
                def _():
                    hop(phase, src, q, CROSS).start()

        first = t - 1

        @pl.when(jnp.logical_and(at_end, jnp.logical_and(first >= 0, first < near)))
        def _():
            hop(phase, beside, first, CROSS).wait_recv()

            @pl.when(z == 0)
            def _():
                hop(phase, beside, first, UP).start()

            @pl.when(z != 0)
            def _():
                hop(phase, beside, first, DOWN).start()

        for sign, onward in ((1, DOWN), (-1, UP)):
            d = deep - 1 - z if sign > 0 else z
            src = (z + sign * d) * WIDE + (1 - x)
            q = t - (PIECES * d + 2 - d)

            @pl.when(
                jnp.logical_and(
                    jnp.logical_and(d > 0, d < deep - 1), jnp.logical_and(q >= 0, q < near)
                )
            )
            def _():
                hop(phase, src, q, CROSS).wait_recv()
                hop(phase, src, q, onward).start()

    def drain(phase):
        def sent(direction, count):
            settled((xs, att)[phase].at[pl.ds(0, count * parts[phase])], ssem.at[phase, direction])

        for at in range(deep):

            @pl.when(z == at)
            def _():
                ends = at in (0, deep - 1)
                sent(CROSS, PIECES * (deep - 1) + (near if ends else 0))
                if at < deep - 1:
                    sent(UP, PIECES * (at + 1) + near)
                if at > 0:
                    sent(DOWN, PIECES * (deep - at) + near)

    def sweep(phase, wait_steps, prepare, use_all, use_half, between):
        steps = (deep - 1) * PIECES
        done = min(steps - wait_steps, len(order) - 3)

        def quiet(t, carry):
            passing(phase, t)
            return carry

        def busy(t, carry):
            item(phase, lookup(order[:done], t - wait_steps), use_all, use_half)
            passing(phase, t)
            return carry

        def rest(i, carry):
            item(phase, lookup(tail, i), use_all, use_half)
            return carry

        tail = order[done:] + far_order
        lax.fori_loop(0, wait_steps, quiet, 0)
        prepare()
        lax.fori_loop(wait_steps, wait_steps + done, busy, 0)
        lax.fori_loop(wait_steps + done, steps, quiet, 0)
        lax.fori_loop(0, len(tail) - 1, rest, 0)
        between()
        lax.fori_loop(len(tail) - 1, len(tail), rest, 0)

    def statistics():
        settled(wq, wq_sem)
        settled(sums.at[pl.ds(0, n - 1), pl.ds(0, 2)], sums_recv)
        settled(mods.at[pl.ds(0, n - 1), pl.ds(0, 2)], mods_recv)
        total = jnp.zeros((1, rows), jnp.float32)
        for p in range(n):
            total = total + sums[p, 0:1, :]
        grand = total * (1.0 / n)
        m2 = jnp.zeros((1, rows), jnp.float32)
        for p in range(n):
            gap = sums[p, 0:1, :] - grand
            m2 = m2 + sums[p, 1:2, :] + feats * (gap * gap)
        inv = lax.rsqrt(m2 * (1.0 / (n * feats)) + 1e-06)
        stat[0] = jnp.broadcast_to(grand, (LANES, rows)).T
        stat[1] = jnp.broadcast_to(inv, (LANES, rows)).T

    def project(src, start, size):
        taken = pl.ds(start, size)
        mean, rstd = stat[0, taken, :], stat[1, taken, :]
        shift = mods[src, 0:1, :].astype(jnp.float32)
        scale = 1.0 + mods[src, 1:2, :].astype(jnp.float32)
        pieces = []
        for c in range(feats // LANES):
            cols = slice(c * LANES, (c + 1) * LANES)
            values = xs[pl.ds(src * rows + start, size), cols].astype(jnp.float32)
            pieces.append(
                ((values - mean) * rstd * scale[:, cols] + shift[:, cols]).astype(jnp.bfloat16)
            )
        acc[taken, :] += jnp.dot(
            jnp.concatenate(pieces, axis=1), wq[src], preferred_element_type=jnp.float32
        )

    sweep(
        0,
        PIECES + PIECES // 2,
        statistics,
        lambda src: project(src, 0, rows),
        lambda src, start: project(src, start, half),
        lambda: None,
    )

    def kv_copy(h):
        return pltpu.make_async_remote_copy(
            src_ref=proj.at[:, pl.ds((3 * h + 1) * HEAD_DIM, 2 * HEAD_DIM)],
            dst_ref=pkv.at[h],
            send_sem=kv_send,
            recv_sem=kv_recv.at[h],
            device_id={"section": other},
            device_id_type=MESH,
        )

    for h in range(heads):
        cols = slice((3 * h + 1) * HEAD_DIM, (3 * h + 3) * HEAD_DIM)
        proj[:, cols] = acc[:, cols].astype(jnp.bfloat16)
        kv_copy(h).start()

    factor = 1.0 / math.sqrt(HEAD_DIM)
    contract = (((1,), (1,)), ((), ()))
    part = parts[1]
    for q in range(PIECES):
        h, taken = q % heads, pl.ds(q // heads * part, part)
        base = 3 * h * HEAD_DIM
        queries = acc[taken, base : base + HEAD_DIM].astype(jnp.bfloat16)
        own_k = proj[:, base + HEAD_DIM : base + 2 * HEAD_DIM]
        own_v = proj[:, base + 2 * HEAD_DIM : base + 3 * HEAD_DIM]
        s_own = lax.dot_general(queries, own_k, contract, preferred_element_type=jnp.float32) * factor
        if q < heads:
            kv_copy(h).wait_recv()
        far_k = pkv[h, :, 0:HEAD_DIM]
        far_v = pkv[h, :, HEAD_DIM : 2 * HEAD_DIM]
        s_far = lax.dot_general(queries, far_k, contract, preferred_element_type=jnp.float32) * factor
        top = jnp.maximum(
            jnp.max(s_own, axis=1, keepdims=True), jnp.max(s_far, axis=1, keepdims=True)
        )
        e_own = jnp.exp(s_own - top)
        e_far = jnp.exp(s_far - top)
        norm = jnp.sum(e_own, axis=1, keepdims=True) + jnp.sum(e_far, axis=1, keepdims=True)
        weighted = jnp.dot(
            e_own.astype(jnp.bfloat16), own_v, preferred_element_type=jnp.float32
        ) + jnp.dot(e_far.astype(jnp.bfloat16), far_v, preferred_element_type=jnp.float32)
        first = pl.multiple_of((me * heads + h) * rows + q // heads * part, part)
        att[pl.ds(first, part), :] = (weighted / norm).astype(jnp.bfloat16)
        hop(1, me, q, CROSS).start()

        @pl.when(jnp.logical_not(at_end))
        def _():
            own_along(1, q)

        if q >= near:

            @pl.when(at_end)
            def _():
                own_along(1, q - near)

    @pl.when(at_end)
    def _():
        for slot in range(near, PIECES):
            own_along(1, slot)

    def settle():
        settled(wo, wo_sem)
        settled(sums.at[pl.ds(0, n - 1), pl.ds(0, 2)], sums_send)
        settled(mods.at[pl.ds(0, n - 1), pl.ds(0, 2)], mods_send)
        settled(wq.at[pl.ds(0, per_sec)], wq_send)
        settled(wo.at[pl.ds(0, per_sec)], wo_send)
        settled(pkv, kv_send)
        drain(0)

    def mix(src, start, size):
        taken = pl.ds(start, size)
        joined = jnp.concatenate(
            [att[pl.ds((src * heads + h) * rows + start, size), :] for h in range(heads)], axis=1
        )
        mixed[taken, :] += jnp.dot(joined, wo[src], preferred_element_type=jnp.float32)

    settle()
    sweep(
        1,
        PIECES + 1,
        lambda: None,
        lambda src: mix(src, 0, rows),
        lambda src, start: mix(src, start, half),
        lambda: drain(1),
    )

    out_ref[...] = (xs[pl.ds(me * rows, rows), :].astype(jnp.float32) + gate[0:1, :] * mixed[...]).astype(jnp.bfloat16)


def fused(n, latent, t_index, mod_table, w_qkv, w_out):
    mod_table = jnp.transpose(mod_table, (1, 0, 2))
    rows, feats = latent.shape
    depth, cols = w_qkv.shape
    depth_o, cols_o = w_out.shape
    heads = cols // (3 * HEAD_DIM)
    bf, f32 = jnp.bfloat16, jnp.float32
    dma = pltpu.SemaphoreType.DMA
    return pl.pallas_call(
        functools.partial(fused_kernel, n),
        out_shape=pltpu.VMEM((rows, feats), bf),
        in_specs=[
            pl.BlockSpec(memory_space=pltpu.HBM),
            pl.BlockSpec(memory_space=pltpu.SMEM),
            pl.BlockSpec(memory_space=pltpu.HBM),
            pl.BlockSpec(memory_space=pltpu.HBM),
            pl.BlockSpec(memory_space=pltpu.HBM),
        ],
        out_specs=pl.BlockSpec(memory_space=pltpu.VMEM),
        scratch_shapes=[
            pltpu.VMEM((n * rows, feats), bf),
            pltpu.VMEM(mod_table.shape, bf),
            pltpu.VMEM((n, 16, feats), bf),
            pltpu.VMEM((n, 8, rows), f32),
            pltpu.VMEM((8, feats), f32),
            pltpu.VMEM((n, 2 * depth // n, cols), bf),
            pltpu.VMEM((n, 2 * depth_o // n, cols_o), bf),
            pltpu.VMEM((rows, cols), f32),
            pltpu.VMEM((2, rows, LANES), f32),
            pltpu.VMEM((rows, cols), bf),
            pltpu.VMEM((heads, rows, 2 * HEAD_DIM), bf),
            pltpu.VMEM((n * heads * rows, HEAD_DIM), bf),
            pltpu.VMEM((rows, cols_o), f32),
            dma,
            dma,
            dma((2, 3)),
            dma((2, n, PIECES)),
            dma,
            dma,
            dma,
            dma,
            dma,
            dma,
            dma,
            dma,
            dma,
            dma((heads,)),
            pltpu.SemaphoreType.REGULAR((3,)),
        ],
        compiler_params=pltpu.CompilerParams(
            collective_id=0, has_side_effects=True, vmem_limit_bytes=24 * 1024 * 1024
        ),
    )(*(pltpu.with_memory_space_constraint(v, pltpu.HBM) if v.ndim > 1 else v for v in (latent, t_index, mod_table, w_qkv, w_out)))


def solution(mesh):
    in_specs = (
        P(("groups", "seq", "section"), "mp"),
        P("groups"),
        P(None, None, "mp"),
        P("section", "mp"),
        P("section", "mp"),
    )
    out_specs = P(("groups", "seq", "section"), "mp")
    n = mesh.shape["mp"]

    def body(latent, t_index, mod_table, w_qkv, w_out):
        heads = w_qkv.shape[1] // (3 * HEAD_DIM)
        fits = (
            mesh.shape["seq"] == 1
            and mesh.shape["section"] == 2
            and n % WIDE == 0
            and n >= 3 * WIDE
            and heads == 2
            and latent.shape[0] <= latent.shape[1]
            and latent.shape[0] % 256 == 0
        )
        if not fits:
            return local(latent, t_index, mod_table, w_qkv, w_out)
        return fused(n, latent, t_index, mod_table, w_qkv, w_out)

    return jax.shard_map(body, mesh=mesh, in_specs=in_specs, out_specs=out_specs, check_vma=False)
```

time: 42.4 us -> 39.3 us (0.927)
  Pallas kernels: 40.9 us -> 37.8 us
    pallas_call x1, Pallas kernels: 40.9 us -> 37.8 us  [fused(): pl.pallas_call(functools.partial(fused_kernel, n), out_shape=pltpu.VMEM((...]
where the time goes in v3:
time: 39.3 us; the launch traced here: 39.1 us
  Pallas kernels  37.8 us (96%)
  local copies, waits for them, and re-layouts  0.68 us (2%)
  between operations  0.66 us (2%)
    pallas_call x1, Pallas kernels, fused(): pl.pallas_call(functools.partial(fused_kernel, n), out_shape=pltpu.VMEM((...  37.8 us

profile of v3, /device:TPU:0, one launch (start us, length us, event | category | flops | bytes accessed | tf_op | source)
XLA Modules:
  0.0 39.1 jit_solution(16116972839018428347)
XLA Ops:
  0.7 37.8 %shard_map.55 = bf16[256,384]{1,0:T(8,128)(2,1)S(1)} custom-call(bf16[256,384]{1,0:T(8,128)(2,1)} %x_hbm.1, s32[1]{0:T(128)S(6)} %copy.8.t_ref, bf16[3,28,384]{2,1,0:T(8,128)(2,1)} %bitcast.1, bf16[1536,768]{1,0:T(8,128)(2,1)} %wq_hbm.1, bf16[1024,384]{1,0:T(8,128)(2,1)} %wo_hbm.1), custom_call_target="tpu_custom_call" | custom-call | tf_op jit(solution)/shard_map/pallas_call | solution.py:637
  38.4 0.7 %copy.7 = bf16[256,384]{1,0:T(8,128)(2,1)} copy(bf16[256,384]{1,0:T(8,128)(2,1)S(1)} %shard_map.55) | data formatting | bytes 393216

commit v4 on v3

--- a/solution.py
+++ b/solution.py
@@ -11,7 +11,7 @@
 HEAD_DIM = 128
 LANES = 128
 WIDE = 2
-PIECES = 4
+PIECES = (4, 8)
 MESH = pl.DeviceIdType.MESH
 
 
@@ -96,11 +96,21 @@
     def pack(d, other, far):
         return (d * 2 + other) * 2 + far
 
-    order = [pack(0, 0, 0), pack(1, 0, 0), pack(0, 1, 0)]
-    for d in range(2, deep):
-        order += [pack(d, 0, 0), pack(d - 1, 1, 0)]
-    order.append(pack(deep - 1, 1, 0))
-    return order, [pack(d, 1, 1) for d in range(1, deep)]
+    me, beside, idle = pack(0, 0, 0), pack(0, 1, 0), pack(deep, 0, 0)
+    own = [pack(d, 0, 0) for d in range(deep)]
+    cross = [pack(d, 1, 0) for d in range(deep)]
+    far = [pack(d, 1, 1) for d in range(deep)]
+    features = (
+        [me, own[1], beside, own[2], cross[1]],
+        [own[3], cross[2], cross[3], far[1], far[2], far[3]],
+    )
+    heads = (
+        ([idle], [me]),
+        ([me, own[1], beside, own[2], cross[1]], [own[1], beside, own[2], cross[1], cross[2]]),
+        ([own[3], cross[2], cross[3]], [far[1], far[2], idle]),
+        ([far[3]], [idle]),
+    )
+    return features, heads
 
 
 def fused_kernel(
@@ -157,6 +167,10 @@
     beside = z * WIDE + (1 - x)
     UP, DOWN, CROSS = 0, 1, 2
     targets = (me + WIDE, me - WIDE, beside)
+    into = jnp.where(2 * z < deep, 1, -1)
+    inward = jnp.where(2 * z < deep, UP, DOWN)
+    outer = jnp.where(2 * z < deep, DOWN, UP)
+    next_in, second_in, next_out = (me + step * into * WIDE for step in (1, 2, -1))
 
     barrier = pltpu.get_barrier_semaphore()
     pl.semaphore_signal(barrier, inc=1, device_id={"mp": beside}, device_id_type=MESH)
@@ -210,29 +224,31 @@
             device_id_type=MESH,
         )
 
-    parts = (rows // PIECES, rows * heads // PIECES)
+    parts = tuple(rows * (1, heads)[phase] // PIECES[phase] for phase in range(2))
+    near_of = tuple(count // 2 for count in PIECES)
+    subs = PIECES[1] // (2 * heads)
 
     def chunk(phase, src, q):
         part = parts[phase]
         if phase == 0:
             return xs.at[pl.ds(pl.multiple_of(src * rows + q * part, part), part), :]
-        first = (src * heads + lax.rem(q, heads)) * rows + q // heads * part
+        block = q // subs
+        first = (src * heads + lax.rem(block, heads)) * rows
+        first += (block // heads * subs + lax.rem(q, subs)) * part
         return att.at[pl.ds(pl.multiple_of(first, part), part), :]
 
-    def hop(phase, src, q, direction):
+    def hop(phase, src, q, direction, target=None):
         return pltpu.make_async_remote_copy(
             src_ref=chunk(phase, src, q),
             dst_ref=chunk(phase, src, q),
             send_sem=ssem.at[phase, direction],
-            recv_sem=rsem.at[phase, src, q],
-            device_id={"mp": targets[direction]},
+            recv_sem=rsem.at[(src * PIECES[0], n * PIECES[0] + src * PIECES[1])[phase] + q],
+            device_id={"mp": targets[direction] if target is None else target},
             device_id_type=MESH,
         )
 
-    near = PIECES // 2
-
     def own_along(phase, slot):
-        q = lax.rem(slot + jnp.where(at_end, near, 0), PIECES)
+        q = lax.rem(slot + jnp.where(at_end, near_of[phase], 0), PIECES[phase])
 
         @pl.when(above)
         def _():
@@ -249,34 +265,26 @@
             wave.at[which], inc=1, device_id={"mp": target}, device_id_type=MESH
         )
 
-    @pl.when(z == 0)
-    def _():
-        tell(UP, me + WIDE)
-
-    @pl.when(z == deep - 1)
-    def _():
-        tell(DOWN, me - WIDE)
-
     def rise():
-        @pl.when(below)
+        @pl.when(z > 1)
         def _():
             pl.semaphore_wait(wave.at[UP], 1)
 
-            @pl.when(above)
-            def _():
-                tell(UP, me + WIDE)
+        @pl.when(jnp.logical_and(below, above))
+        def _():
+            tell(UP, me + WIDE)
 
     def sink():
-        @pl.when(above)
+        @pl.when(z < deep - 2)
         def _():
             pl.semaphore_wait(wave.at[DOWN], 1)
 
-            @pl.when(below)
-            def _():
-                tell(DOWN, me - WIDE)
+        @pl.when(jnp.logical_and(below, above))
+        def _():
+            tell(DOWN, me - WIDE)
 
     own_copy.wait()
-    for slot in range(PIECES - 1):
+    for slot in range(PIECES[0] - 1):
         hop(0, me, slot, CROSS).start()
         own_along(0, slot)
 
@@ -343,8 +351,8 @@
     for step in range(1, n):
         for copy in small_copies(step):
             copy.start()
-    hop(0, me, PIECES - 1, CROSS).start()
-    own_along(0, PIECES - 1)
+    hop(0, me, PIECES[0] - 1, CROSS).start()
+    own_along(0, PIECES[0] - 1)
     for i in range(per_sec):
         wq_remote(i).start()
     for i in range(per_sec):
@@ -353,7 +361,7 @@
     acc[...] = jnp.zeros_like(acc)
     mixed[...] = jnp.zeros_like(mixed)
 
-    order, far_order = item_codes(deep)
+    feature_items, head_items = item_codes(deep)
 
     def lookup(table_of, j):
         found = table_of[0]
@@ -368,12 +376,13 @@
         return jnp.logical_or(sz == 0, sz == deep - 1)
 
     def item(phase, code, use_all, use_half):
+        count, near = PIECES[phase], near_of[phase]
         far = lax.rem(code, 2) == 1
         crossed = lax.rem(code // 2, 2) == 1
         d = code // 4
 
         def one(i, carry):
-            sz = z + (1 - 2 * i) * d
+            sz = z + (1 - 2 * i) * into * d
             end = is_end(sz)
             src = sz * WIDE + jnp.where(crossed, 1 - x, x)
             valid = jnp.logical_and(inside(sz), jnp.logical_or(jnp.logical_not(far), end))
@@ -382,15 +391,23 @@
 
             @pl.when(direct)
             def _():
-                for q in range(near, PIECES):
+                for q in range(near, count):
                     hop(phase, src, q, CROSS).wait_recv()
 
-            @pl.when(jnp.logical_and(direct, jnp.logical_not(end)))
+            whole = jnp.logical_and(direct, jnp.logical_not(end))
+            if phase == 1:
+                whole = jnp.logical_and(whole, d > 0)
+
+            @pl.when(whole)
             def _():
                 for q in range(near):
                     hop(phase, src, q, CROSS).wait_recv()
 
-            @pl.when(jnp.logical_and(jnp.logical_and(valid, far), d == deep - 1))
+            unseen = d == deep - 1
+            if phase == 1:
+                unseen = d != deep - 2
+
+            @pl.when(jnp.logical_and(jnp.logical_and(valid, far), unseen))
             def _():
                 for q in range(near):
                     hop(phase, src, q, CROSS).wait_recv()
@@ -407,57 +424,92 @@
 
             return carry
 
-        lax.fori_loop(0, 2, one, 0)
-
-    def passing(phase, t):
-        s, slot = 1 + t // PIECES, lax.rem(t, PIECES)
+        lax.fori_loop(0, jnp.where(at_end, 1, 2), one, 0)
+
+    def passing(t):
+        count, near = PIECES[0], near_of[0]
+        s, slot = 1 + t // count, lax.rem(t, count)
         for sign, onward, has in ((1, DOWN, below), (-1, UP, above)):
             sz = z + sign * s
             src = sz * WIDE + x
             end = is_end(sz)
-            q = lax.rem(slot + jnp.where(end, near, 0), PIECES)
+            q = lax.rem(slot + jnp.where(end, near, 0), count)
 
             @pl.when(inside(sz))
             def _():
-                hop(phase, src, q, CROSS).wait_recv()
+                hop(0, src, q, CROSS).wait_recv()
 
                 @pl.when(has)
                 def _():
-                    hop(phase, src, q, onward).start()
+                    hop(0, src, q, onward).start()
 
                 @pl.when(jnp.logical_not(jnp.logical_and(q < near, end)))
                 def _():
-                    hop(phase, src, q, CROSS).start()
+                    hop(0, src, q, CROSS).start()
 
         first = t - 1
 
         @pl.when(jnp.logical_and(at_end, jnp.logical_and(first >= 0, first < near)))
         def _():
-            hop(phase, beside, first, CROSS).wait_recv()
-
-            @pl.when(z == 0)
-            def _():
-                hop(phase, beside, first, UP).start()
-
-            @pl.when(z != 0)
-            def _():
-                hop(phase, beside, first, DOWN).start()
+            hop(0, beside, first, CROSS).wait_recv()
+            hop(0, beside, first, inward, me + into * WIDE).start()
 
         for sign, onward in ((1, DOWN), (-1, UP)):
             d = deep - 1 - z if sign > 0 else z
             src = (z + sign * d) * WIDE + (1 - x)
-            q = t - (PIECES * d + 2 - d)
-
-            @pl.when(
-                jnp.logical_and(
-                    jnp.logical_and(d > 0, d < deep - 1), jnp.logical_and(q >= 0, q < near)
-                )
-            )
+            q = t - (count * d + 2 - d)
+            passed = jnp.logical_and(d > 0, d < deep - 1)
+
+            @pl.when(jnp.logical_and(passed, jnp.logical_and(q >= 0, q < near)))
             def _():
-                hop(phase, src, q, CROSS).wait_recv()
-                hop(phase, src, q, onward).start()
+                hop(0, src, q, CROSS).wait_recv()
+                hop(0, src, q, onward).start()
+
+    def pass_on(sz, column, turns, to=(), across=()):
+        src = sz * WIDE + column
+        for q in turns:
+            hop(1, src, q, CROSS).wait_recv()
+            for direction, target in to:
+                hop(1, src, q, direction, target).start()
+            if q in across:
+                hop(1, src, q, CROSS).start()
+
+    every = list(range(PIECES[1]))
+    far_half, near_half = every[: near_of[1]], every[near_of[1] :]
+    to_next, to_second, to_outer = (inward, next_in), (inward, second_in), (outer, next_out)
+
+    def relay_first():
+        @pl.when(at_end)
+        def _():
+            pass_on(z + into, x, near_half, across=near_half)
+            for one in far_half:
+                pass_on(z, 1 - x, [one], to=[to_second])
+                pass_on(z + into, x, [one])
+            for q in near_half:
+                hop(1, me, q, *to_next).start()
+            for q in far_half:
+                hop(1, beside, q, *to_next).start()
+            pass_on(z + 2 * into, x, every, across=every)
+
+        @pl.when(jnp.logical_not(at_end))
+        def _():
+            pass_on(z + into, x, every, to=[to_outer], across=every)
+            pass_on(z, 1 - x, far_half, to=[to_outer])
+            pass_on(z - into, x, far_half, to=[to_next])
+            pass_on(z + 2 * into, x, near_half, to=[to_outer], across=near_half)
+            for one in far_half:
+                pass_on(z + 2 * into, x, [one], to=[to_outer])
+                pass_on(z + 2 * into, 1 - x, [one], to=[to_outer])
+            pass_on(z - into, x, near_half, across=near_half)
+
+    def relay_last():
+        @pl.when(at_end)
+        def _():
+            pass_on(z + 3 * into, x, near_half + far_half, across=near_half)
 
     def drain(phase):
+        pieces, near = PIECES[phase], near_of[phase]
+
         def sent(direction, count):
             settled((xs, att)[phase].at[pl.ds(0, count * parts[phase])], ssem.at[phase, direction])
 
@@ -466,37 +518,60 @@
             @pl.when(z == at)
             def _():
                 ends = at in (0, deep - 1)
-                sent(CROSS, PIECES * (deep - 1) + (near if ends else 0))
+                if phase == 0:
+                    sent(CROSS, pieces * (deep - 1) + (near if ends else 0))
+                else:
+                    sent(CROSS, pieces * (deep - 1))
+                if phase == 0:
+                    up, down = pieces * (at + 1) + near, pieces * (deep - at) + near
+                elif ends:
+                    up = down = pieces + near + 2 * near
+                else:
+                    along = (pieces + near, 3 * pieces + 2 * near)
+                    up, down = along if 2 * at < deep else along[::-1]
                 if at < deep - 1:
-                    sent(UP, PIECES * (at + 1) + near)
+                    sent(UP, up)
                 if at > 0:
-                    sent(DOWN, PIECES * (deep - at) + near)
-
-    def sweep(phase, wait_steps, prepare, use_all, use_half, between):
-        steps = (deep - 1) * PIECES
-        done = min(steps - wait_steps, len(order) - 3)
+                    sent(DOWN, down)
+
+    def run(phase, items, use_all, use_half):
+        end_items, middle_items = items
+
+        def one(i, carry):
+            code = jnp.where(at_end, lookup(end_items, i), lookup(middle_items, i))
+            item(phase, code, use_all, use_half)
+            return carry
+
+        lax.fori_loop(0, len(end_items), one, 0)
+
+    def gather_features(use_all, use_half):
+        steps, wait_steps = (deep - 1) * PIECES[0], PIECES[0] + PIECES[0] // 2
+        items, tail = feature_items
 
         def quiet(t, carry):
-            passing(phase, t)
+            passing(t)
             return carry
 
         def busy(t, carry):
-            item(phase, lookup(order[:done], t - wait_steps), use_all, use_half)
-            passing(phase, t)
+            item(0, lookup(items, t - wait_steps), use_all, use_half)
+            passing(t)
             return carry
 
-        def rest(i, carry):
-            item(phase, lookup(tail, i), use_all, use_half)
-            return carry
-
-        tail = order[done:] + far_order
+        until = wait_steps + len(items)
         lax.fori_loop(0, wait_steps, quiet, 0)
-        prepare()
-        lax.fori_loop(wait_steps, wait_steps + done, busy, 0)
-        lax.fori_loop(wait_steps + done, steps, quiet, 0)
-        lax.fori_loop(0, len(tail) - 1, rest, 0)
-        between()
-        lax.fori_loop(len(tail) - 1, len(tail), rest, 0)
+        statistics()
+        lax.fori_loop(wait_steps, until, busy, 0)
+        lax.fori_loop(until, steps, quiet, 0)
+        run(0, (tail, tail), use_all, use_half)
+
+    def gather_heads(use_all, use_half):
+        run(1, head_items[0], use_all, use_half)
+        relay_first()
+        run(1, head_items[1], use_all, use_half)
+        relay_last()
+        run(1, head_items[2], use_all, use_half)
+        drain(1)
+        run(1, head_items[3], use_all, use_half)
 
     def statistics():
         settled(wq, wq_sem)
@@ -530,13 +605,8 @@
             jnp.concatenate(pieces, axis=1), wq[src], preferred_element_type=jnp.float32
         )
 
-    sweep(
-        0,
-        PIECES + PIECES // 2,
-        statistics,
-        lambda src: project(src, 0, rows),
-        lambda src, start: project(src, start, half),
-        lambda: None,
+    gather_features(
+        lambda src: project(src, 0, rows), lambda src, start: project(src, start, half)
     )
 
     def kv_copy(h):
@@ -556,15 +626,14 @@
 
     factor = 1.0 / math.sqrt(HEAD_DIM)
     contract = (((1,), (1,)), ((), ()))
-    part = parts[1]
-    for q in range(PIECES):
-        h, taken = q % heads, pl.ds(q // heads * part, part)
+    for block in range(2 * heads):
+        h, taken = block % heads, pl.ds(block // heads * half, half)
         base = 3 * h * HEAD_DIM
         queries = acc[taken, base : base + HEAD_DIM].astype(jnp.bfloat16)
         own_k = proj[:, base + HEAD_DIM : base + 2 * HEAD_DIM]
         own_v = proj[:, base + 2 * HEAD_DIM : base + 3 * HEAD_DIM]
         s_own = lax.dot_general(queries, own_k, contract, preferred_element_type=jnp.float32) * factor
-        if q < heads:
+        if block < heads:
             kv_copy(h).wait_recv()
         far_k = pkv[h, :, 0:HEAD_DIM]
         far_v = pkv[h, :, HEAD_DIM : 2 * HEAD_DIM]
@@ -578,24 +647,22 @@
         weighted = jnp.dot(
             e_own.astype(jnp.bfloat16), own_v, preferred_element_type=jnp.float32
         ) + jnp.dot(e_far.astype(jnp.bfloat16), far_v, preferred_element_type=jnp.float32)
-        first = pl.multiple_of((me * heads + h) * rows + q // heads * part, part)
-        att[pl.ds(first, part), :] = (weighted / norm).astype(jnp.bfloat16)
-        hop(1, me, q, CROSS).start()
+        first = pl.multiple_of((me * heads + h) * rows + block // heads * half, half)
+        att[pl.ds(first, half), :] = (weighted / norm).astype(jnp.bfloat16)
+        turn = range(block * subs, (block + 1) * subs)
+        for q in turn:
+            hop(1, me, q, CROSS).start()
 
         @pl.when(jnp.logical_not(at_end))
         def _():
-            own_along(1, q)
-
-        if q >= near:
-
-            @pl.when(at_end)
-            def _():
-                own_along(1, q - near)
-
-    @pl.when(at_end)
-    def _():
-        for slot in range(near, PIECES):
-            own_along(1, slot)
+            for q in turn:
+                hop(1, me, q, *to_next).start()
+                hop(1, me, q, *to_outer).start()
+
+        @pl.when(at_end)
+        def _():
+            for q in turn:
+                hop(1, me, q, *(to_next if block < heads else to_second)).start()
 
     def settle():
         settled(wo, wo_sem)
@@ -614,14 +681,7 @@
         mixed[taken, :] += jnp.dot(joined, wo[src], preferred_element_type=jnp.float32)
 
     settle()
-    sweep(
-        1,
-        PIECES + 1,
-        lambda: None,
-        lambda src: mix(src, 0, rows),
-        lambda src, start: mix(src, start, half),
-        lambda: drain(1),
-    )
+    gather_heads(lambda src: mix(src, 0, rows), lambda src, start: mix(src, start, half))
 
     out_ref[...] = (xs[pl.ds(me * rows, rows), :].astype(jnp.float32) + gate[0:1, :] * mixed[...]).astype(jnp.bfloat16)
 
@@ -662,7 +722,7 @@
             dma,
             dma,
             dma((2, 3)),
-            dma((2, n, PIECES)),
+            dma((n * sum(PIECES),)),
             dma,
             dma,
             dma,
@@ -698,7 +758,7 @@
             mesh.shape["seq"] == 1
             and mesh.shape["section"] == 2
             and n % WIDE == 0
-            and n >= 3 * WIDE
+            and n == 4 * WIDE
             and heads == 2
             and latent.shape[0] <= latent.shape[1]
             and latent.shape[0] % 256 == 0

time: 39.3 us -> 38.2 us (0.972)
  Pallas kernels: 37.8 us -> 36.8 us
    pallas_call x1, Pallas kernels: 37.8 us -> 36.8 us  [fused(): pl.pallas_call(functools.partial(fused_kernel, n), out_shape=pltpu.VMEM((...]
where the time goes in v4:
time: 38.2 us; the launch traced here: 38.1 us
  Pallas kernels  36.8 us (96%)
  local copies, waits for them, and re-layouts  0.68 us (2%)
  between operations  0.66 us (2%)
    pallas_call x1, Pallas kernels, fused(): pl.pallas_call(functools.partial(fused_kernel, n), out_shape=pltpu.VMEM((...  36.8 us

profile of v4, /device:TPU:0, one launch (start us, length us, event | category | flops | bytes accessed | tf_op | source)
XLA Modules:
  0.0 38.1 jit_solution(7075589133208861641)
XLA Ops:
  0.7 36.8 %shard_map.55 = bf16[256,384]{1,0:T(8,128)(2,1)S(1)} custom-call(bf16[256,384]{1,0:T(8,128)(2,1)} %x_hbm.1, s32[1]{0:T(128)S(6)} %copy.8.t_ref, bf16[3,28,384]{2,1,0:T(8,128)(2,1)} %bitcast.1, bf16[1536,768]{1,0:T(8,128)(2,1)} %wq_hbm.1, bf16[1024,384]{1,0:T(8,128)(2,1)} %wo_hbm.1), custom_call_target="tpu_custom_call" | custom-call | tf_op jit(solution)/shard_map/pallas_call | solution.py:697
  37.4 0.7 %copy.7 = bf16[256,384]{1,0:T(8,128)(2,1)} copy(bf16[256,384]{1,0:T(8,128)(2,1)S(1)} %shard_map.55) | data formatting | bytes 393216

commit v5 on v4

--- a/solution.py
+++ b/solution.py
@@ -107,8 +107,8 @@
     heads = (
         ([idle], [me]),
         ([me, own[1], beside, own[2], cross[1]], [own[1], beside, own[2], cross[1], cross[2]]),
-        ([own[3], cross[2], cross[3]], [far[1], far[2], idle]),
-        ([far[3]], [idle]),
+        ([cross[2], own[3], pack(3, 0, 1), far[3]], [far[1], far[2], idle, idle]),
+        ([cross[3]], [idle]),
     )
     return features, heads
 
@@ -184,8 +184,16 @@
     def _():
         pl.semaphore_signal(barrier, inc=1, device_id={"mp": me - WIDE}, device_id_type=MESH)
 
-    own_copy = pltpu.make_async_copy(x_hbm, xs.at[pl.ds(me * rows, rows)], own_sem)
-    own_copy.start()
+    def own_copy(q):
+        part = rows // PIECES[0]
+        return pltpu.make_async_copy(
+            x_hbm.at[pl.ds(q * part, part)],
+            xs.at[pl.ds(pl.multiple_of(me * rows + q * part, part), part)],
+            own_sem.at[q],
+        )
+
+    for q in range(PIECES[0]):
+        own_copy(q).start()
     table_copy = pltpu.make_async_copy(mod_hbm, table, table_sem)
     table_copy.start()
 
@@ -283,8 +291,10 @@
         def _():
             tell(DOWN, me - WIDE)
 
-    own_copy.wait()
     for slot in range(PIECES[0] - 1):
+        if slot < near_of[0]:
+            own_copy(slot).wait()
+            own_copy(slot + near_of[0]).wait()
         hop(0, me, slot, CROSS).start()
         own_along(0, slot)
 
@@ -412,7 +422,10 @@
                 for q in range(near):
                     hop(phase, src, q, CROSS).wait_recv()
 
-            split = jnp.logical_and(crossed, jnp.logical_and(end, d > 0))
+            halved = crossed
+            if phase == 1:
+                halved = jnp.logical_or(crossed, d == deep - 1)
+            split = jnp.logical_and(halved, jnp.logical_and(end, d > 0))
 
             @pl.when(jnp.logical_and(valid, jnp.logical_not(split)))
             def _():
@@ -505,7 +518,7 @@
     def relay_last():
         @pl.when(at_end)
         def _():
-            pass_on(z + 3 * into, x, near_half + far_half, across=near_half)
+            pass_on(z + 3 * into, x, near_half, across=near_half)
 
     def drain(phase):
         pieces, near = PIECES[phase], near_of[phase]
@@ -624,32 +637,47 @@
         proj[:, cols] = acc[:, cols].astype(jnp.bfloat16)
         kv_copy(h).start()
 
-    factor = 1.0 / math.sqrt(HEAD_DIM)
+    factor = math.log2(math.e) / math.sqrt(HEAD_DIM)
     contract = (((1,), (1,)), ((), ()))
-    for block in range(2 * heads):
-        h, taken = block % heads, pl.ds(block // heads * half, half)
-        base = 3 * h * HEAD_DIM
-        queries = acc[taken, base : base + HEAD_DIM].astype(jnp.bfloat16)
-        own_k = proj[:, base + HEAD_DIM : base + 2 * HEAD_DIM]
-        own_v = proj[:, base + 2 * HEAD_DIM : base + 3 * HEAD_DIM]
-        s_own = lax.dot_general(queries, own_k, contract, preferred_element_type=jnp.float32) * factor
-        if block < heads:
-            kv_copy(h).wait_recv()
-        far_k = pkv[h, :, 0:HEAD_DIM]
-        far_v = pkv[h, :, HEAD_DIM : 2 * HEAD_DIM]
-        s_far = lax.dot_general(queries, far_k, contract, preferred_element_type=jnp.float32) * factor
-        top = jnp.maximum(
-            jnp.max(s_own, axis=1, keepdims=True), jnp.max(s_far, axis=1, keepdims=True)
-        )
-        e_own = jnp.exp(s_own - top)
-        e_far = jnp.exp(s_far - top)
-        norm = jnp.sum(e_own, axis=1, keepdims=True) + jnp.sum(e_far, axis=1, keepdims=True)
-        weighted = jnp.dot(
-            e_own.astype(jnp.bfloat16), own_v, preferred_element_type=jnp.float32
-        ) + jnp.dot(e_far.astype(jnp.bfloat16), far_v, preferred_element_type=jnp.float32)
-        first = pl.multiple_of((me * heads + h) * rows + block // heads * half, half)
-        att[pl.ds(first, half), :] = (weighted / norm).astype(jnp.bfloat16)
-        turn = range(block * subs, (block + 1) * subs)
+    def attend(taken):
+        raw, tops, sides = [], [], []
+        for h in range(heads):
+            base = 3 * h * HEAD_DIM
+            queries = acc[taken, base : base + HEAD_DIM].astype(jnp.bfloat16)
+            own_k = proj[:, base + HEAD_DIM : base + 2 * HEAD_DIM]
+            far_k = pkv[h, :, 0:HEAD_DIM]
+            raw.append(
+                [
+                    lax.dot_general(queries, keys, contract, preferred_element_type=jnp.float32)
+                    for keys in (own_k, far_k)
+                ]
+            )
+        for own_s, far_s in raw:
+            tops.append(
+                jnp.maximum(
+                    jnp.max(own_s, axis=1, keepdims=True), jnp.max(far_s, axis=1, keepdims=True)
+                )
+            )
+        for pair, top in zip(raw, tops):
+            sides.append([jnp.exp2((scores - top) * factor) for scores in pair])
+        results = []
+        for h, (e_own, e_far) in enumerate(sides):
+            base = 3 * h * HEAD_DIM
+            own_v = proj[:, base + 2 * HEAD_DIM : base + 3 * HEAD_DIM]
+            far_v = pkv[h, :, HEAD_DIM : 2 * HEAD_DIM]
+            norm = jnp.sum(e_own, axis=1, keepdims=True) + jnp.sum(e_far, axis=1, keepdims=True)
+            weighted = jnp.dot(
+                e_own.astype(jnp.bfloat16), own_v, preferred_element_type=jnp.float32
+            ) + jnp.dot(e_far.astype(jnp.bfloat16), far_v, preferred_element_type=jnp.float32)
+            results.append((weighted / norm).astype(jnp.bfloat16))
+        return results
+
+    for h in range(heads):
+        kv_copy(h).wait_recv()
+    for turn, first_half in ((far_half, True), (near_half, False)):
+        start = 0 if first_half else half
+        for h, result in enumerate(attend(pl.ds(start, half))):
+            att[pl.ds(pl.multiple_of((me * heads + h) * rows + start, half), half), :] = result
         for q in turn:
             hop(1, me, q, CROSS).start()
 
@@ -662,7 +690,7 @@
         @pl.when(at_end)
         def _():
             for q in turn:
-                hop(1, me, q, *(to_next if block < heads else to_second)).start()
+                hop(1, me, q, *(to_next if first_half else to_second)).start()
 
     def settle():
         settled(wo, wo_sem)
@@ -719,7 +747,7 @@
             pltpu.VMEM((heads, rows, 2 * HEAD_DIM), bf),
             pltpu.VMEM((n * heads * rows, HEAD_DIM), bf),
             pltpu.VMEM((rows, cols_o), f32),
-            dma,
+            dma((PIECES[0],)),
             dma,
             dma((2, 3)),
             dma((n * sum(PIECES),)),

time: 38.2 us -> 38.1 us (level)
  no operation moved by 1% of the time
where the time goes in v5:
time: 38.1 us; the launch traced here: 37.9 us
  Pallas kernels  36.6 us (96%)
  local copies, waits for them, and re-layouts  0.68 us (2%)
  between operations  0.66 us (2%)
    pallas_call x1, Pallas kernels, fused(): pl.pallas_call(functools.partial(fused_kernel, n), out_shape=pltpu.VMEM((...  36.6 us

profile of v5, /device:TPU:0, one launch (start us, length us, event | category | flops | bytes accessed | tf_op | source)
XLA Modules:
  0.0 37.9 jit_solution(1902079727126861158)
XLA Ops:
  0.7 36.6 %shard_map.55 = bf16[256,384]{1,0:T(8,128)(2,1)S(1)} custom-call(bf16[256,384]{1,0:T(8,128)(2,1)} %x_hbm.1, s32[1]{0:T(128)S(6)} %copy.8.t_ref, bf16[3,28,384]{2,1,0:T(8,128)(2,1)} %bitcast.1, bf16[1536,768]{1,0:T(8,128)(2,1)} %wq_hbm.1, bf16[1024,384]{1,0:T(8,128)(2,1)} %wo_hbm.1), custom_call_target="tpu_custom_call" | custom-call | tf_op jit(solution)/shard_map/pallas_call | solution.py:725
  37.3 0.7 %copy.7 = bf16[256,384]{1,0:T(8,128)(2,1)} copy(bf16[256,384]{1,0:T(8,128)(2,1)S(1)} %shard_map.55) | data formatting | bytes 393216

commit v6 on v5

--- a/solution.py
+++ b/solution.py
@@ -245,15 +245,28 @@
         first += (block // heads * subs + lax.rem(q, subs)) * part
         return att.at[pl.ds(pl.multiple_of(first, part), part), :]
 
+    def arrival(phase, src, q, column):
+        count, near = PIECES[phase], near_of[phase]
+        row = src // WIDE
+        along = row * count + q
+        crossed = deep * count + row * (near + 1) + jnp.minimum(q, near)
+        base = phase * deep * (PIECES[0] + near_of[0] + 1)
+        return rsem.at[base + jnp.where(src % WIDE == column, along, crossed)]
+
     def hop(phase, src, q, direction, target=None):
+        column = 1 - x if target is None and direction == CROSS else x
         return pltpu.make_async_remote_copy(
             src_ref=chunk(phase, src, q),
             dst_ref=chunk(phase, src, q),
             send_sem=ssem.at[phase, direction],
-            recv_sem=rsem.at[(src * PIECES[0], n * PIECES[0] + src * PIECES[1])[phase] + q],
+            recv_sem=arrival(phase, src, q, column),
             device_id={"mp": targets[direction] if target is None else target},
             device_id_type=MESH,
         )
+
+    def landed(phase, src, q):
+        piece = chunk(phase, src, q)
+        return pltpu.make_async_copy(piece, piece, arrival(phase, src, q, x))
 
     def own_along(phase, slot):
         q = lax.rem(slot + jnp.where(at_end, near_of[phase], 0), PIECES[phase])
@@ -401,8 +414,8 @@
 
             @pl.when(direct)
             def _():
-                for q in range(near, count):
-                    hop(phase, src, q, CROSS).wait_recv()
+                block = (xs, att)[phase].at[pl.ds(0, near * parts[phase])]
+                settled(block, arrival(phase, src, near, x))
 
             whole = jnp.logical_and(direct, jnp.logical_not(end))
             if phase == 1:
@@ -411,7 +424,7 @@
             @pl.when(whole)
             def _():
                 for q in range(near):
-                    hop(phase, src, q, CROSS).wait_recv()
+                    landed(phase, src, q).wait()
 
             unseen = d == deep - 1
             if phase == 1:
@@ -420,7 +433,7 @@
             @pl.when(jnp.logical_and(jnp.logical_and(valid, far), unseen))
             def _():
                 for q in range(near):
-                    hop(phase, src, q, CROSS).wait_recv()
+                    landed(phase, src, q).wait()
 
             halved = crossed
             if phase == 1:
@@ -450,7 +463,7 @@
 
             @pl.when(inside(sz))
             def _():
-                hop(0, src, q, CROSS).wait_recv()
+                landed(0, src, q).wait()
 
                 @pl.when(has)
                 def _():
@@ -464,7 +477,7 @@
 
         @pl.when(jnp.logical_and(at_end, jnp.logical_and(first >= 0, first < near)))
         def _():
-            hop(0, beside, first, CROSS).wait_recv()
+            landed(0, beside, first).wait()
             hop(0, beside, first, inward, me + into * WIDE).start()
 
         for sign, onward in ((1, DOWN), (-1, UP)):
@@ -475,13 +488,13 @@
 
             @pl.when(jnp.logical_and(passed, jnp.logical_and(q >= 0, q < near)))
             def _():
-                hop(0, src, q, CROSS).wait_recv()
+                landed(0, src, q).wait()
                 hop(0, src, q, onward).start()
 
     def pass_on(sz, column, turns, to=(), across=()):
         src = sz * WIDE + column
         for q in turns:
-            hop(1, src, q, CROSS).wait_recv()
+            landed(1, src, q).wait()
             for direction, target in to:
                 hop(1, src, q, direction, target).start()
             if q in across:
@@ -558,7 +571,7 @@
         lax.fori_loop(0, len(end_items), one, 0)
 
     def gather_features(use_all, use_half):
-        steps, wait_steps = (deep - 1) * PIECES[0], PIECES[0] + PIECES[0] // 2
+        steps, wait_steps = (deep - 1) * PIECES[0], PIECES[0] + PIECES[0] - 1
         items, tail = feature_items
 
         def quiet(t, carry):
@@ -750,7 +763,7 @@
             dma((PIECES[0],)),
             dma,
             dma((2, 3)),
-            dma((n * sum(PIECES),)),
+            dma((n // WIDE * sum(count + count // 2 + 1 for count in PIECES),)),
             dma,
             dma,
             dma,

time: 38.1 us -> 37.9 us (level)
  no operation moved by 1% of the time
where the time goes in v6:
time: 37.9 us; the launch traced here: 37.7 us
  Pallas kernels  36.3 us (96%)
  local copies, waits for them, and re-layouts  0.68 us (2%)
  between operations  0.66 us (2%)
    pallas_call x1, Pallas kernels, fused(): pl.pallas_call(functools.partial(fused_kernel, n), out_shape=pltpu.VMEM((...  36.3 us

profile of v6, /device:TPU:0, one launch (start us, length us, event | category | flops | bytes accessed | tf_op | source)
XLA Modules:
  0.0 37.7 jit_solution(8477172290356343449)
XLA Ops:
  0.7 36.3 %shard_map.55 = bf16[256,384]{1,0:T(8,128)(2,1)S(1)} custom-call(bf16[256,384]{1,0:T(8,128)(2,1)} %x_hbm.1, s32[1]{0:T(128)S(6)} %copy.8.t_ref, bf16[3,28,384]{2,1,0:T(8,128)(2,1)} %bitcast.1, bf16[1536,768]{1,0:T(8,128)(2,1)} %wq_hbm.1, bf16[1024,384]{1,0:T(8,128)(2,1)} %wo_hbm.1), custom_call_target="tpu_custom_call" | custom-call | tf_op jit(solution)/shard_map/pallas_call | solution.py:738
  37.0 0.7 %copy.7 = bf16[256,384]{1,0:T(8,128)(2,1)} copy(bf16[256,384]{1,0:T(8,128)(2,1)S(1)} %shard_map.55) | data formatting | bytes 393216
